TPU v7x, 32 devices: a whole 2x2x4 slice. The times are simulated.
32 devices in a mesh: shard: 8 (over z, x), tensor: 4 (over y, core).
Axes of the slice: x: 2, y: 2, z: 4, core: 2. Of those that a mesh axis runs over, the one named last changes fastest.
Arguments:
- tokens: bfloat16 [8192, 1024], P('shard'), may hold values from -6 to 6
- cotangent: bfloat16 [8192, 1024], P('shard'), may hold values from -6 to 6
- ln_gain: bfloat16 [2, 2, 1024], P(None, None, 'shard'), may hold values from 0.25 to 1.75
- ln_bias: bfloat16 [2, 2, 1024], P(None, None, 'shard'), may hold values from -1.75 to 1.75
- w_qkv: bfloat16 [2, 1024, 3072], P(None, 'shard', 'tensor'), may hold values from -0.25 to 0.25
- b_qkv: bfloat16 [2, 3072], P(None, ('tensor', 'shard')), may hold values from -1.75 to 1.75
- w_dense: bfloat16 [2, 1024, 1024], P(None, 'tensor', 'shard'), may hold values from -0.5 to 0.5
- b_dense: bfloat16 [2, 1024], P(None, 'shard'), may hold values from -1.75 to 1.75
- w_fc1: bfloat16 [2, 1024, 4096], P(None, 'shard', 'tensor'), may hold values from -0.1875 to 0.1875
- b_fc1: bfloat16 [2, 4096], P(None, ('tensor', 'shard')), may hold values from -1.75 to 1.75
- w_fc2: bfloat16 [2, 4096, 1024], P(None, 'tensor', 'shard'), may hold values from -0.125 to 0.125
- b_fc2: bfloat16 [2, 1024], P(None, 'shard'), may hold values from -1.75 to 1.75
Outputs:
- output: bfloat16 [8192, 1024], P('shard')
- d_tokens: bfloat16 [8192, 1024], P('shard')
- d_ln_gain: float32 [2, 2, 1024], P(None, None, 'shard')
- d_ln_bias: float32 [2, 2, 1024], P(None, None, 'shard')
- d_w_qkv: float32 [2, 1024, 3072], P(None, 'shard', 'tensor')
- d_b_qkv: float32 [2, 3072], P(None, ('tensor', 'shard'))
- d_w_dense: float32 [2, 1024, 1024], P(None, 'tensor', 'shard')
- d_b_dense: float32 [2, 1024], P(None, 'shard')
- d_w_fc1: float32 [2, 1024, 4096], P(None, 'shard', 'tensor')
- d_b_fc1: float32 [2, 4096], P(None, ('tensor', 'shard'))
- d_w_fc2: float32 [2, 4096, 1024], P(None, 'tensor', 'shard')
- d_b_fc2: float32 [2, 1024], P(None, 'shard')
All inputs are finite; a program needn't handle non-finite values.
Results may differ from a plain program's by a relative error of at most 0.04.
Values may be sent and summed in bfloat16 or wider, within the bound.
No kernel may reach another device: no remote copies, remote signals or barrier semaphores. Data moves between devices by JAX's collectives and lax.ppermute only.
A program may use at most 192 MiB of HBM per device.

v0:
```python
import functools
import math

import jax
import jax.numpy as jnp
from jax import lax
from jax.experimental import pallas as pl
from jax.experimental.pallas import tpu as pltpu
from jax.sharding import PartitionSpec as P

HD = 64
ROT = 16
LAYERS = 2
LEN = 512
EXTRA = 16
BF = jnp.bfloat16
F32 = jnp.float32
NT = (((1,), (1,)), ((), ()))
TN = (((0,), (0,)), ((), ()))
VMEM_LIMIT = 56 * 1024 * 1024


def shape(dims, dtype=BF):
    return jax.ShapeDtypeStruct(dims, dtype)


def whole(dims):
    return pl.BlockSpec(dims, lambda *_: (0,) * len(dims))


def call(kernel, out_shape, grid=None, flops=0, moved=0, **kw):
    params = pltpu.CompilerParams(vmem_limit_bytes=VMEM_LIMIT)
    cost = pl.CostEstimate(flops=int(flops), bytes_accessed=int(moved), transcendentals=0)
    if grid is not None:
        kw["grid"] = grid
    return pl.pallas_call(
        kernel, out_shape=out_shape, compiler_params=params, cost_estimate=cost, **kw
    )


def ring_order(count):
    return list(range(0, count, 2)) + list(range(count - 1, 0, -2))


def ring_perms(count):
    order = ring_order(count)
    ahead = [(order[i], order[(i + 1) % count]) for i in range(count)]
    return ahead, [(b, a) for a, b in ahead]


def after(value, *others):
    return lax.optimization_barrier((value,) + others)[0]


def assemble_kernel(count, rows, owner, *refs):
    pieces, out, rest = refs[: count + 1], refs[count + 1], refs[count + 2 :]
    half = out.shape[2] // 2
    far = count // 2
    for step in range(count):
        if step == far:
            continue
        piece = pieces[step if step < far else step + 1]
        out[owner[step]] = piece[:rows]
    out[owner[far], :, :half] = pieces[far][:rows]
    out[owner[far], :, half:] = pieces[far + 1][:rows]
    if rest:
        tail = pieces[0][rows:].astype(F32)
        for step in range(1, count):
            if step != far:
                tail = tail + pieces[step if step < far else step + 1][rows:].astype(F32)
        other = jnp.concatenate([pieces[far][rows:], pieces[far + 1][rows:]], axis=1)
        rest[0][...] = tail + other.astype(F32)


def add_first_kernel(_, left, right, up_piece, down_piece, up, down):
    half = left.shape[1]
    up[:, :half] = (up_piece[0, :, :half].astype(F32) + left[...].astype(F32)).astype(BF)
    up[:, half:] = up_piece[0, :, half:]
    down[:, :half] = down_piece[0, :, :half]
    down[:, half:] = (down_piece[0, :, half:].astype(F32) + right[...].astype(F32)).astype(BF)


def add_kernel(_, up_in, down_in, up_piece, down_piece, up, down):
    up[...] = (up_piece[0].astype(F32) + up_in[...].astype(F32)).astype(BF)
    down[...] = (down_piece[0].astype(F32) + down_in[...].astype(F32)).astype(BF)


def add_last_kernel(_, up_in, down_in, piece, out):
    out[...] = piece[0].astype(F32) + (up_in[...].astype(F32) + down_in[...].astype(F32))


class Ring:
    def __init__(self):
        self.count = lax.axis_size("shard")
        self.order = ring_order(self.count)
        self.ahead, self.back = ring_perms(self.count)
        table = [0] * self.count
        for place, device in enumerate(self.order):
            table[device] = place
        me = lax.axis_index("shard")
        place = jnp.array(table, jnp.int32)[me]
        steps = jnp.arange(self.count, dtype=jnp.int32)
        self.owner = jnp.array(self.order, jnp.int32)[(place + steps) % self.count]
        self.me = me

    def gather(self, part, rows, gate=None):
        count, cols = self.count, part.shape[1]
        half, far = cols // 2, self.count // 2
        if gate is not None:
            part = after(part, gate)
        up = down = part
        pieces = [part] + [None] * count
        for step in range(1, far):
            up = lax.ppermute(up, "shard", self.ahead)
            down = lax.ppermute(down, "shard", self.back)
            pieces[count + 1 - step] = up
            pieces[step] = down
        gate = (up, down)
        pieces[far] = lax.ppermute(up[:, :half], "shard", self.ahead)
        pieces[far + 1] = lax.ppermute(down[:, half:], "shard", self.back)
        outs = [shape((count, rows, cols))]
        if part.shape[0] > rows:
            outs.append(shape((part.shape[0] - rows, cols), F32))
        result = call(
            functools.partial(assemble_kernel, count, rows),
            outs,
            moved=4 * count * rows * cols,
            in_specs=[pl.BlockSpec(memory_space=pltpu.SMEM)]
            + [pl.BlockSpec(memory_space=pltpu.VMEM)] * (count + 1),
        )(self.owner, *pieces)
        return [result[0].reshape(count * rows, cols)] + list(result[1:]), gate

    def scatter(self, total):
        count, rows, cols = total.shape
        half, far = cols // 2, count // 2

        def add(kernel, ups, chosen, outs):
            def place(which):
                return pl.BlockSpec((1, rows, cols), lambda i, own: (own[which], 0, 0))

            return pl.pallas_call(
                kernel,
                out_shape=outs,
                grid_spec=pltpu.PrefetchScalarGridSpec(
                    num_scalar_prefetch=1,
                    grid=(1,),
                    in_specs=[whole(item.shape) for item in ups] + [place(c) for c in chosen],
                    out_specs=[whole(item.shape) for item in outs],
                ),
                compiler_params=pltpu.CompilerParams(vmem_limit_bytes=VMEM_LIMIT),
                cost_estimate=pl.CostEstimate(
                    flops=0, bytes_accessed=12 * rows * cols, transcendentals=0
                ),
            )(self.owner, *ups, *([total] * len(chosen)))

        head = lax.dynamic_index_in_dim(total, self.owner[far], 0, False)
        left = lax.ppermute(head[:, :half], "shard", self.ahead)
        right = lax.ppermute(head[:, half:], "shard", self.back)
        pair = [shape((rows, cols))] * 2
        up, down = add(add_first_kernel, (left, right), (far - 1, far + 1), pair)
        for step in range(far - 1, 0, -1):
            up = lax.ppermute(up, "shard", self.ahead)
            down = lax.ppermute(down, "shard", self.back)
            if step > 1:
                up, down = add(add_kernel, (up, down), (step - 1, count - step + 1), pair)
        return add(add_last_kernel, (up, down), (0,), [shape((rows, cols), F32)])[0]


def partner(bit):
    count = lax.axis_size("tensor")
    return [(i, i ^ (1 << bit)) for i in range(count)]


def tensor_bits():
    return lax.axis_size("tensor").bit_length() - 1


def tensor_scatter(part):
    me = lax.axis_index("tensor")
    first = None
    for bit in range(tensor_bits()):
        rows = part.shape[0] // 2
        side = (me >> bit) & 1
        keep = lax.dynamic_slice_in_dim(part, side * rows, rows, 0)
        give = lax.dynamic_slice_in_dim(part, (1 - side) * rows, rows, 0)
        got = lax.ppermute(give.astype(BF), "tensor", partner(bit))
        first = got if first is None else first
        part = keep.astype(F32) + got.astype(F32)
    return part[0], first


def tensor_own(part):
    me = lax.axis_index("tensor")
    for bit in range(tensor_bits()):
        rows = part.shape[0] // 2
        part = lax.dynamic_slice_in_dim(part, ((me >> bit) & 1) * rows, rows, 0)
    return part[0]


def tensor_gather(part):
    me = lax.axis_index("tensor")
    part = part[None]
    for bit in reversed(range(tensor_bits())):
        got = lax.ppermute(part, "tensor", partner(bit))
        side = (me >> bit) & 1
        part = jnp.where(
            side == 0, jnp.concatenate([part, got], axis=0), jnp.concatenate([got, part], axis=0)
        )
    return part


def tensor_small_sum(value):
    count = lax.axis_size("tensor")
    total = value
    for step in range(1, count):
        total = total + lax.ppermute(value, "tensor", [(i, i ^ step) for i in range(count)])
    return total


def rotate_tables():
    half = ROT // 2
    places = jnp.arange(LEN).astype(F32)
    freqs = jnp.exp(-(2.0 * jnp.arange(half).astype(F32) / ROT) * math.log(10000.0))
    angles = freqs[:, None] * places[None, :]
    return jnp.cos(angles), jnp.sin(angles)


def column(row):
    return jnp.transpose(jnp.broadcast_to(row, (8, row.shape[1])))[:, :1]


def pack_kernel(norms, own, w_qkv, w_up, w_dense, w_down, *outs):
    heads = w_qkv.shape[2] // (3 * HD)
    qkv_cols, up_cols = w_qkv.shape[2], w_up.shape[2]
    mix_cols = qkv_cols // 3
    rows = w_qkv.shape[1]
    tail = []
    for layer in range(LAYERS):
        raw = w_qkv[layer]
        by_kind = jnp.concatenate(
            [
                raw[:, (h * 3 + kind) * HD : (h * 3 + kind + 1) * HD]
                for kind in range(3)
                for h in range(heads)
            ],
            axis=1,
        )
        up = w_up[layer]
        gains = [column(norms[2 * layer + k : 2 * layer + k + 1, :]) for k in range(2)]
        shifts = [norms[4 + 2 * layer + k : 5 + 2 * layer + k, :] for k in range(2)]
        scaled = [
            (mat.astype(F32) * gain).astype(BF) for mat, gain in zip((by_kind, up), gains)
        ]
        moved = [
            jnp.dot(
                jnp.broadcast_to(row, (16, rows)).astype(BF), mat, preferred_element_type=F32
            )[:1]
            for mat, row in zip((by_kind, up), shifts)
        ]
        total = own[layer : layer + 1, :]
        pad = total.shape[1] - qkv_cols - up_cols
        total = total + jnp.concatenate(moved + [jnp.zeros((1, pad), F32)], axis=1)
        high = total.astype(BF).astype(F32)
        for value in (high, total - high):
            for at in range(0, total.shape[1], qkv_cols):
                tail.append(value[:, at : at + qkv_cols])
        first, second, at = (outs[0], outs[1], 0) if layer == 0 else (outs[2], outs[2], qkv_cols)
        first[:rows, :qkv_cols] = scaled[0]
        second[:, at : at + up_cols] = scaled[1]
        at += up_cols
        second[:, at : at + mix_cols] = w_dense[layer].astype(F32).T.astype(BF)
        second[:, at + mix_cols :] = w_down[layer].astype(F32).T.astype(BF)
    outs[0][rows:, :] = jnp.concatenate(tail, axis=0).astype(BF)


def attend_kernel(x, mat, bias, cosine, sine, qkv, mixed, log_total, turned):
    @pl.when(pl.program_id(0) == 0)
    def _():
        turned[...] = mat[:, : turned.shape[0]].T

    seq = jnp.concatenate([x[b] for b in range(x.shape[0])], axis=1)
    joined = jnp.dot(turned[...], seq, preferred_element_type=F32) + column(bias[...])
    part = joined.shape[0] // 3
    heads = part // HD
    half = ROT // 2
    cos, sin = cosine[...], sine[...]
    for kind in range(2):
        for h in range(heads):
            at = kind * part + h * HD
            low, high = joined[at : at + half], joined[at + half : at + ROT]
            turn = jnp.concatenate([low * cos - high * sin, high * cos + low * sin], axis=0)
            qkv[at : at + ROT, :] = turn.astype(BF)
            qkv[at + ROT : at + HD, :] = joined[at + ROT : at + HD].astype(BF)
    qkv[2 * part :, :] = joined[2 * part :].astype(BF)
    wide = LEN // 2
    log_total[...] = jnp.zeros_like(log_total)
    for h in range(heads):
        for q_at in range(0, LEN, wide):
            keys = q_at + wide
            query = qkv[h * HD : (h + 1) * HD, q_at:keys]
            key = qkv[part + h * HD : part + (h + 1) * HD, :keys]
            value = qkv[2 * part + h * HD : 2 * part + (h + 1) * HD, :keys]
            scores = masked_scores(key, query, q_at)
            highest = jnp.max(scores, axis=0, keepdims=True)
            chances = jnp.exp(scores - highest)
            total = jnp.sum(chances, axis=0, keepdims=True)
            out = jnp.dot(value, chances.astype(BF), preferred_element_type=F32)
            for b in range(wide // mixed.shape[2]):
                cut = slice(b * mixed.shape[2], (b + 1) * mixed.shape[2])
                at = q_at // mixed.shape[2] + b
                mixed[at, h * HD : (h + 1) * HD, :] = (out / total)[:, cut].astype(BF)
            log_total[h : h + 1, q_at:keys] = highest + jnp.log(total)


def masked_scores(key, query, q_at):
    scores = lax.dot_general(key, query, TN, preferred_element_type=F32) * (1.0 / math.sqrt(HD))
    key_at = lax.broadcasted_iota(jnp.int32, scores.shape, 0)
    query_at = lax.broadcasted_iota(jnp.int32, scores.shape, 1) + q_at
    return jnp.where(query_at >= key_at, scores, -1e30)


def attend_back_kernel(qkv, log_total, d_mixed, cosine, sine, d_joined, grads):
    part = qkv.shape[0] // 3
    heads = part // HD
    half = ROT // 2
    wide = LEN // 2
    block = d_mixed.shape[2]
    scale = 1.0 / math.sqrt(HD)
    cos, sin = cosine[...], sine[...]
    for h in range(heads):
        d_key, d_value = [], []
        for q_at in range(0, LEN, wide):
            keys = q_at + wide
            query = qkv[h * HD : (h + 1) * HD, q_at:keys]
            key = qkv[part + h * HD : part + (h + 1) * HD, :keys]
            value = qkv[2 * part + h * HD : 2 * part + (h + 1) * HD, :keys]
            d_out = jnp.concatenate(
                [
                    d_mixed[q_at // block + b, h * HD : (h + 1) * HD, :]
                    for b in range(wide // block)
                ],
                axis=1,
            )
            scores = masked_scores(key, query, q_at)
            chances = jnp.exp(scores - log_total[h : h + 1, q_at:keys])
            d_chances = lax.dot_general(value, d_out, TN, preferred_element_type=F32)
            weighted = chances * d_chances
            inner = jnp.sum(weighted, axis=0, keepdims=True)
            d_scores = (weighted - chances * inner).astype(BF)
            grads[h * HD : (h + 1) * HD, q_at:keys] = (
                jnp.dot(key, d_scores, preferred_element_type=F32) * scale
            )
            d_key.append(lax.dot_general(query, d_scores, NT, preferred_element_type=F32))
            d_value.append(
                lax.dot_general(d_out, chances.astype(BF), NT, preferred_element_type=F32)
            )
        for base, items, factor in ((part, d_key, scale), (2 * part, d_value, 1.0)):
            at = base + h * HD
            grads[at : at + HD, :wide] = (items[0] + items[1][:, :wide]) * factor
            grads[at : at + HD, wide:] = items[1][:, wide:] * factor
    whole_grad = grads[...]
    pieces = []
    for kind in range(2):
        for h in range(heads):
            at = kind * part + h * HD
            low, high = whole_grad[at : at + half], whole_grad[at + half : at + ROT]
            pieces += [low * cos + high * sin, high * cos - low * sin]
            pieces.append(whole_grad[at + ROT : at + HD])
    pieces.append(whole_grad[2 * part :])
    result = jnp.concatenate(pieces, axis=0).astype(BF)
    for b in range(LEN // block):
        d_joined[b] = result[:, b * block : (b + 1) * block]


def gelu_both(hidden_in):
    normal_cdf = 0.5 * (1.0 + lax.erf(hidden_in * (1.0 / math.sqrt(2.0))))
    density = jnp.exp(-0.5 * hidden_in * hidden_in) * (1.0 / math.sqrt(2.0 * math.pi))
    return hidden_in * normal_cdf, normal_cdf + hidden_in * density


def widen_kernel(at, x, mat, bias, hidden, slope, turned):
    @pl.when(pl.program_id(0) == 0)
    def _():
        turned[...] = mat[:, at : at + turned.shape[0]].T

    hidden_in = jnp.dot(turned[...], x[0], preferred_element_type=F32) + column(bias[...])
    value, rise = gelu_both(hidden_in)
    hidden[0] = value.astype(BF)
    slope[0] = rise.astype(BF)


def branch_kernel(at, mixed, hidden, mat, out):
    cut = at + mixed.shape[1]
    out[0] = (
        jnp.dot(mat[:, at:cut], mixed[0], preferred_element_type=F32)
        + jnp.dot(mat[:, cut:], hidden[0], preferred_element_type=F32)
    ).astype(BF)


def narrow_kernel(at, grad, mat, slope, d_mixed, d_hidden, turned):
    @pl.when(pl.program_id(0) == 0)
    def _():
        turned[...] = mat[:, at:].T

    cut = d_mixed.shape[1]
    both = jnp.dot(turned[...], grad[0], preferred_element_type=F32)
    d_mixed[0] = both[:cut].astype(BF)
    d_hidden[0] = (both[cut:] * slope[0].astype(F32)).astype(BF)


def shaped_kernel(at, d_joined, d_hidden, qkv_mat, up_mat, out):
    cut, end = d_joined.shape[1], at + d_hidden.shape[1]
    out[0] = (
        jnp.dot(qkv_mat[:, :cut], d_joined[0], preferred_element_type=F32)
        + jnp.dot(up_mat[:, at:end], d_hidden[0], preferred_element_type=F32)
    ).astype(BF)


def lanes(ref):
    return jnp.concatenate([ref[b] for b in range(ref.shape[0])], axis=1)


def grad_kernel(pairs, sums, *refs):
    ins, out = refs[:-1], refs[-1]
    chunks = out.shape[0]
    rows = out.shape[1] - (EXTRA if sums else 0)
    lo = 0
    for left, right in pairs:
        width = ins[right].shape[1]
        got = lax.dot_general(
            lanes(ins[left]), lanes(ins[right]), NT, preferred_element_type=F32
        ).astype(BF)
        out[:, :rows, lo : lo + width] = got.reshape(chunks, rows, width)
        lo += width
    if sums:
        total = []
        for item in sums:
            right = lanes(ins[item])
            ones = jnp.ones((16, right.shape[1]), BF)
            total.append(lax.dot_general(ones, right, NT, preferred_element_type=F32)[:1])
        qkv_cols = ins[sums[0]].shape[1]
        used = sum(item.shape[1] for item in total)
        total = jnp.concatenate(total + [jnp.zeros((1, 4 * qkv_cols - used), F32)], axis=1)
        tail = [total[:, at : at + qkv_cols] for at in range(0, 4 * qkv_cols, qkv_cols)]
        tail = jnp.concatenate(tail + [jnp.zeros((EXTRA - 4, qkv_cols), F32)], axis=0).astype(BF)
        for c in range(chunks):
            out[c, rows:, :qkv_cols] = tail
            if out.shape[2] > qkv_cols:
                out[c, rows:, qkv_cols:] = jnp.zeros((EXTRA, out.shape[2] - qkv_cols), BF)


def finish_kernel(layer, split, norms, w_qkv, w_up, *refs):
    parts, outs = refs[: 1 + split], refs[-6:]
    d_qkv, d_up, d_dense, d_down, d_norm, sums = outs
    rows, qkv_cols = w_qkv.shape[1], w_qkv.shape[2]
    up_cols, mix_cols = w_up.shape[2], d_dense.shape[1]
    heads = qkv_cols // (3 * HD)
    got = parts[0][:rows, :qkv_cols].astype(F32)
    tail = parts[0][rows:, :qkv_cols].astype(F32)
    rest = parts[1][...] if split else parts[0][:rows, qkv_cols:].astype(F32)
    total = jnp.concatenate([tail[r : r + 1] for r in range(4)], axis=1)
    sums[0] = total
    gains = [column(norms[2 * layer + k : 2 * layer + k + 1, :]) for k in range(2)]
    shifts = [column(norms[4 + 2 * layer + k : 5 + 2 * layer + k, :]) for k in range(2)]
    raw = w_qkv[0].astype(F32)
    full = gains[0] * got + shifts[0] * total[:, :qkv_cols]
    gain_sum = jnp.zeros((rows, 1), F32)
    shift_sum = jnp.zeros((rows, 1), F32)
    for h in range(heads):
        for kind in range(3):
            to, at = (h * 3 + kind) * HD, (kind * heads + h) * HD
            d_qkv[0, :, to : to + HD] = full[:, at : at + HD]
            piece = raw[:, to : to + HD]
            gain_sum += jnp.sum(piece * got[:, at : at + HD], axis=1, keepdims=True)
            shift_sum += jnp.sum(piece * total[:, at : at + HD], axis=1, keepdims=True)
    up_sum = total[:, qkv_cols : qkv_cols + up_cols]
    raw = w_up[0].astype(F32)
    d_up[0] = gains[1] * rest[:, :up_cols] + shifts[1] * up_sum
    columns = [
        gain_sum,
        jnp.sum(raw * rest[:, :up_cols], axis=1, keepdims=True),
        shift_sum,
        jnp.sum(raw * up_sum, axis=1, keepdims=True),
        jnp.zeros((rows, 4), F32),
    ]
    d_norm[0] = jnp.transpose(jnp.concatenate(columns, axis=1))
    d_dense[0] = jnp.transpose(rest[:, up_cols : up_cols + mix_cols])
    d_down[0] = jnp.transpose(rest[:, up_cols + mix_cols :])


def normalize(resid):
    centered = resid - jnp.mean(resid, axis=-2, keepdims=True)
    factor = lax.rsqrt(jnp.mean(centered * centered, axis=-2, keepdims=True) + 1e-05)
    return (centered * factor, factor)


def by_head(mat):
    lead, cols = mat.shape[:-1], mat.shape[-1]
    mat = mat.reshape(lead + (3, cols // (3 * HD), HD))
    return jnp.swapaxes(mat, -3, -2).reshape(lead + (cols,))


def by_kind(mat):
    lead, cols = mat.shape[:-1], mat.shape[-1]
    mat = mat.reshape(lead + (cols // (3 * HD), 3, HD))
    return jnp.swapaxes(mat, -3, -2).reshape(lead + (cols,))


def per_device(
    tokens, cotangent, ln_gain, ln_bias, w_qkv, b_qkv, w_dense, b_dense, w_fc1, b_fc1, w_fc2, b_fc2
):
    token_count, model = tokens.shape
    rows = w_qkv.shape[1]
    qkv_cols, ff_cols = w_qkv.shape[2], w_fc1.shape[2]
    mix_cols = qkv_cols // 3
    in_cols, out_cols = qkv_cols + ff_cols, mix_cols + ff_cols
    blocks = lax.axis_size("tensor")
    block = token_count // blocks
    seqs, seq_blocks = token_count // LEN, LEN // block
    ring = Ring()
    count, me = ring.count, ring.me
    tables = rotate_tables()
    gains, shifts = ln_gain.astype(F32), ln_bias.astype(F32)

    small = 4 * qkv_cols
    own = jnp.concatenate(
        [
            by_kind(
                lax.dynamic_update_slice(
                    jnp.zeros((LAYERS, qkv_cols), F32),
                    b_qkv.astype(F32),
                    (0, me * b_qkv.shape[1]),
                )
            ),
            lax.dynamic_update_slice(
                jnp.zeros((LAYERS, ff_cols), F32), b_fc1.astype(F32), (0, me * b_fc1.shape[1])
            ),
            lax.dynamic_update_slice(
                jnp.zeros((LAYERS, small - in_cols), F32),
                b_dense.astype(F32) + b_fc2.astype(F32),
                (0, me * b_dense.shape[1]),
            ),
        ],
        axis=1,
    )
    norms = jnp.concatenate([gains.reshape(4, rows), shifts.reshape(4, rows)], axis=0)
    rest_cols = ff_cols + out_cols
    packed = call(
        pack_kernel,
        [
            shape((rows + EXTRA, qkv_cols)),
            shape((rows, rest_cols)),
            shape((rows, in_cols + out_cols)),
        ],
        moved=8 * rows * (in_cols + out_cols),
    )(norms, own, w_qkv, w_fc1, w_dense, w_fc2)
    (qkv_0, tail), gate = ring.gather(packed[0], rows)
    all_1 = lax.all_gather(after(packed[2], gate), "shard", axis=0, tiled=True)
    (rest_0,), gate = ring.gather(packed[1], rows, gate)
    mats = [
        ((qkv_0, 0), (rest_0, 0), (rest_0, ff_cols)),
        ((all_1, 0), (all_1, qkv_cols), (all_1, in_cols)),
    ]
    tail = tail.reshape(LAYERS, 2, small)
    biases = tail[:, 0] + tail[:, 1]

    def turn(item):
        return jnp.swapaxes(item.reshape(blocks, block, item.shape[1]), 1, 2)

    def unturn(item):
        return jnp.swapaxes(item, 1, 2).reshape(token_count, model)

    def per_block(features):
        return pl.BlockSpec((1, features, block), lambda i: (i, 0, 0))

    def per_seq(features):
        return pl.BlockSpec((seq_blocks, features, block), lambda i: (i, 0, 0))

    def seq_lanes(features):
        return pl.BlockSpec((features, LEN), lambda i: (0, i))

    half_rot = ROT // 2
    block_of = lambda features: whole((blocks, features, block))

    def attend(normed, layer):
        mat, _ = mats[layer][0]
        return call(
            attend_kernel,
            [
                shape((qkv_cols, token_count)),
                shape((blocks, mix_cols, block)),
                shape((8, token_count), F32),
            ],
            grid=(seqs,),
            flops=2 * token_count * (model * qkv_cols + 2 * LEN * mix_cols),
            moved=2 * model * (token_count + qkv_cols),
            in_specs=[
                per_seq(model),
                whole((model, qkv_cols)),
                whole((1, qkv_cols)),
                whole((half_rot, LEN)),
                whole((half_rot, LEN)),
            ],
            out_specs=[seq_lanes(qkv_cols), per_seq(mix_cols), seq_lanes(8)],
            scratch_shapes=[pltpu.VMEM((qkv_cols, model), BF)],
        )(normed, mat, biases[layer : layer + 1, :qkv_cols], *tables)

    def widen(normed, layer):
        mat, at = mats[layer][1]
        return call(
            functools.partial(widen_kernel, at),
            [shape((blocks, ff_cols, block))] * 2,
            grid=(blocks,),
            flops=2 * token_count * model * ff_cols,
            moved=2 * model * (token_count + ff_cols) + 4 * token_count * ff_cols,
            in_specs=[per_block(model), whole(mat.shape), whole((1, ff_cols))],
            out_specs=[per_block(ff_cols)] * 2,
            scratch_shapes=[pltpu.VMEM((ff_cols, model), BF)],
        )(normed, mat, biases[layer : layer + 1, qkv_cols:in_cols])

    def branch_of(mixed, hidden, layer):
        mat, at = mats[layer][2]
        return call(
            functools.partial(branch_kernel, at),
            shape((blocks, model, block)),
            grid=(blocks,),
            flops=2 * token_count * model * out_cols,
            moved=2 * model * (token_count + out_cols) + 2 * token_count * out_cols,
            in_specs=[per_block(mix_cols), per_block(ff_cols), whole(mat.shape)],
            out_specs=per_block(model),
        )(mixed, hidden, mat)

    def narrow(grad_low, slope, layer):
        mat, at = mats[layer][2]
        return call(
            functools.partial(narrow_kernel, at),
            [shape((blocks, mix_cols, block)), shape((blocks, ff_cols, block))],
            grid=(blocks,),
            flops=2 * token_count * model * out_cols,
            moved=2 * model * (token_count + out_cols) + 4 * token_count * out_cols,
            in_specs=[per_block(model), whole(mat.shape), per_block(ff_cols)],
            out_specs=[per_block(mix_cols), per_block(ff_cols)],
            scratch_shapes=[pltpu.VMEM((out_cols, model), BF)],
        )(grad_low, mat, slope)

    def attend_back(qkv, log_total, d_mixed):
        return call(
            attend_back_kernel,
            shape((blocks, qkv_cols, block)),
            grid=(seqs,),
            flops=10 * token_count * LEN * mix_cols,
            moved=6 * token_count * qkv_cols,
            in_specs=[
                seq_lanes(qkv_cols),
                seq_lanes(8),
                per_seq(mix_cols),
                whole((half_rot, LEN)),
                whole((half_rot, LEN)),
            ],
            out_specs=per_seq(qkv_cols),
            scratch_shapes=[pltpu.VMEM((qkv_cols, LEN), F32)],
        )(qkv, log_total, d_mixed, *tables)

    def shaped_of(d_joined, d_hidden, layer):
        (qkv_mat, _), (up_mat, at) = mats[layer][:2]
        return call(
            functools.partial(shaped_kernel, at),
            shape((blocks, model, block)),
            grid=(blocks,),
            flops=2 * token_count * model * in_cols,
            moved=2 * model * (token_count + in_cols) + 2 * token_count * in_cols,
            in_specs=[
                per_block(qkv_cols),
                per_block(ff_cols),
                whole((model, qkv_cols)),
                whole(up_mat.shape),
            ],
            out_specs=per_block(model),
        )(d_joined, d_hidden, qkv_mat, up_mat)

    def grads_of(pairs, sums, *items):
        parts = 2
        lefts = {left for left, _ in pairs}
        cols = sum(items[right].shape[1] for _, right in pairs)
        high = rows + (EXTRA if sums else 0)
        return call(
            functools.partial(grad_kernel, pairs, sums),
            shape((count, high, cols)),
            grid=(parts,),
            flops=2 * token_count * model * cols,
            moved=2 * model * (token_count + cols) + 2 * token_count * cols,
            in_specs=[
                pl.BlockSpec((blocks, model // parts, block), lambda i: (0, i, 0))
                if k in lefts
                else block_of(item.shape[1])
                for k, item in enumerate(items)
            ],
            out_specs=pl.BlockSpec((count // parts, high, cols), lambda i: (i, 0, 0)),
        )(*items)

    def grad_step(grad, shaped, own_normed, factor):
        return grad + factor * (
            shaped
            - jnp.mean(shaped, axis=0, keepdims=True)
            - own_normed * jnp.mean(shaped * own_normed, axis=0, keepdims=True)
        )

    token_blocks = turn(tokens).astype(F32)
    resid_0 = tensor_own(token_blocks)
    own_normed_0, factor_0 = normalize(resid_0)
    normed_0 = normalize(token_blocks)[0].astype(BF)
    qkv_rows_0, mixed_0, log_0 = attend(normed_0, 0)
    hidden_0, slope_0 = widen(normed_0, 0)
    branch, _ = tensor_scatter(branch_of(mixed_0, hidden_0, 0))
    resid_1 = resid_0 + branch + biases[0, in_cols : in_cols + model][:, None]
    own_normed_1, factor_1 = normalize(resid_1)
    normed_1 = tensor_gather(own_normed_1.astype(BF))
    qkv_rows_1, mixed_1, log_1 = attend(normed_1, 1)
    hidden_1, slope_1 = widen(normed_1, 1)

    grad_low_2 = turn(cotangent)
    d_mixed, d_hidden = narrow(grad_low_2, slope_1, 1)
    d_joined = attend_back(qkv_rows_1, log_1, d_mixed)
    shaped, met = tensor_scatter(shaped_of(d_joined, d_hidden, 1))
    total_1 = grads_of(
        ((0, 2), (0, 3), (1, 4), (1, 5)),
        (2, 3, 6),
        after(normed_1, met),
        grad_low_2,
        d_joined,
        d_hidden,
        mixed_1,
        hidden_1,
        grad_low_2,
    )
    sum_1 = lax.psum_scatter(total_1, "shard", scatter_dimension=0, tiled=True)[0]
    grad_1 = grad_step(tensor_own(grad_low_2).astype(F32), shaped, own_normed_1, factor_1)
    grad_low_1 = tensor_gather(grad_1.astype(BF))

    branch, _ = tensor_scatter(branch_of(mixed_1, after(hidden_1, total_1), 1))
    resid_2 = resid_1 + branch + biases[1, in_cols : in_cols + model][:, None]
    output = tensor_gather(resid_2.astype(BF))

    d_mixed, d_hidden = narrow(grad_low_1, slope_0, 0)
    rest_sum = ring.scatter(
        grads_of(((0, 2), (1, 3), (1, 4)), (), normed_0, grad_low_1, d_hidden, mixed_0, hidden_0)
    )
    d_joined = attend_back(qkv_rows_0, log_0, d_mixed)
    qkv_sum = ring.scatter(
        grads_of(((0, 1),), (1, 2, 3), normed_0, d_joined, d_hidden, grad_low_1)
    )
    shaped, _ = tensor_scatter(shaped_of(d_joined, d_hidden, 0))
    grad_0 = grad_step(grad_1, shaped, own_normed_0, factor_0)
    grad_low_0 = tensor_gather(grad_0.astype(BF))

    def finish(layer, parts, kept):
        def at(dims):
            return pl.BlockSpec((1,) + dims, lambda i: (layer, 0, 0))

        outs = [
            (rows, qkv_cols), (rows, ff_cols), w_dense.shape[1:], w_fc2.shape[1:], (8, rows),
            (1, small),
        ]
        first = 3 + len(parts)
        return call(
            functools.partial(finish_kernel, layer, len(parts) - 1),
            [shape((LAYERS,) + item, F32) for item in outs],
            grid=(1,),
            moved=8 * rows * (in_cols + out_cols),
            in_specs=[whole(norms.shape), at((rows, qkv_cols)), at((rows, ff_cols))]
            + [whole(item.shape) for item in parts]
            + [pl.BlockSpec(memory_space=pl.ANY)] * len(kept),
            out_specs=[at(item) for item in outs],
            input_output_aliases={first + k: k for k in range(len(kept))},
        )(norms, w_qkv, w_fc1, *parts, *kept)

    kept = finish(1, (sum_1,), ())
    d_qkv, d_up, d_dense, d_down, d_norm, sums = finish(0, (qkv_sum, rest_sum), kept)
    d_norm = tensor_small_sum(d_norm)
    sums = sums[:, 0]
    d_out_bias = lax.dynamic_slice(
        sums, (0, in_cols + me * b_dense.shape[1]), b_dense.shape
    )
    return (
        unturn(output),
        unturn(grad_low_0),
        d_norm[:, :2],
        d_norm[:, 2:4],
        d_qkv,
        lax.dynamic_slice(by_head(sums[:, :qkv_cols]), (0, me * b_qkv.shape[1]), b_qkv.shape),
        d_dense,
        d_out_bias,
        d_up,
        lax.dynamic_slice(sums, (0, qkv_cols + me * b_fc1.shape[1]), b_fc1.shape),
        d_down,
        d_out_bias,
    )


def solution(mesh):
    in_specs = (
        P("shard", None),
        P("shard", None),
        P(None, None, "shard"),
        P(None, None, "shard"),
        P(None, "shard", "tensor"),
        P(None, ("tensor", "shard")),
        P(None, "tensor", "shard"),
        P(None, "shard"),
        P(None, "shard", "tensor"),
        P(None, ("tensor", "shard")),
        P(None, "tensor", "shard"),
        P(None, "shard"),
    )
    out_specs = (
        P("shard", None),
        P("shard", None),
        P(None, None, "shard"),
        P(None, None, "shard"),
        P(None, "shard", "tensor"),
        P(None, ("tensor", "shard")),
        P(None, "tensor", "shard"),
        P(None, "shard"),
        P(None, "shard", "tensor"),
        P(None, ("tensor", "shard")),
        P(None, "tensor", "shard"),
        P(None, "shard"),
    )
    return jax.shard_map(
        per_device, mesh=mesh, in_specs=in_specs, out_specs=out_specs, check_vma=False
    )
```

profile of v0, /device:TPU:0, one launch (start us, length us, event | category | flops | bytes accessed | tf_op | source)
XLA Modules:
  0.0 564.9 jit_solution(18231989335510764369)
XLA Ops:
  10.9 3.0 shard_map.229
  13.9 3.1 collective-permute-start
  17.1 5.6 collective-permute-done.refs_1_
  24.8 4.6 collective-permute-done.1.refs_2_
  31.4 3.9 collective-permute-done.2.refs_3_
  36.7 3.0 copy.33
  40.4 2.6 bitcast_reduce_fusion
  52.8 22.3 %collective-permute-done.6.refs_4_ = bf16[144,384]{1,0:T(8,128)(2,1)S(1)} collective-permute-done((bf16[144,384]{1,0:T(8,128)(2,1)S(1)}, bf16[144,384]{1,0:T(8,128)(2,1)S(1)}, u32[]{:S(2)}, u32[]{:S(2)}) %collective-permute-start.6) | collective-permute-done | bytes 110624 | tf_op jit(solution)/shard_map/ppermute | solution.py:119
  75.1 12.1 %collective-permute-done.7.refs_5_ = bf16[144,384]{1,0:T(8,128)(2,1)S(1)} collective-permute-done((bf16[144,384]{1,0:T(8,128)(2,1)S(1)}, bf16[144,384]{1,0:T(8,128)(2,1)S(1)}, u32[]{:S(2)}, u32[]{:S(2)}) %collective-permute-start.7) | collective-permute-done | bytes 110624 | tf_op jit(solution)/shard_map/ppermute | solution.py:120
  87.9 2.9 shard_map.230
  93.7 39.6 %collective-permute-done.9.refs_2_ = bf16[128,2304]{1,0:T(8,128)(2,1)S(1)} collective-permute-done((bf16[128,2304]{1,0:T(8,128)(2,1)S(1)}, bf16[128,2304]{1,0:T(8,128)(2,1)S(1)}, u32[]{:S(2)}, u32[]{:S(2)}) %collective-permute-start.9) | collective-permute-done | bytes 589856 | tf_op jit(solution)/shard_map/ppermute | solution.py:115
  133.3 2.0 collective-permute-start.13
  136.0 17.8 %collective-permute-done.13.refs_6_ = bf16[128,2304]{1,0:T(8,128)(2,1)S(1)} collective-permute-done((bf16[128,2304]{1,0:T(8,128)(2,1)S(1)}, bf16[128,2304]{1,0:T(8,128)(2,1)S(1)}, u32[]{:S(2)}, u32[]{:S(2)}) %collective-permute-start.13) | collective-permute-done | bytes 589856 | tf_op jit(solution)/shard_map/ppermute | solution.py:114
  153.8 12.8 %collective-permute-start.14 = (bf16[128,1152]{1,0:T(8,128)(2,1)S(1)}, bf16[128,1152]{1,0:T(8,128)(2,1)S(1)}, u32[]{:S(2)}, u32[]{:S(2)}) collective-permute-start(bf16[128,1152]{1,0:T(8,128)(2,1)S(1)} %slice.94), channel_id=1, source_target_pairs={{0,8},{8,16},{16,24},{24,28},{28,20},{20,12},{12,4},{4,0},{1,9},{9... | collective-permute-start | bytes 884744 | tf_op jit(solution)/shard_map/ppermute | solution.py:119
  167.2 1.9 collective-permute-start.15
  169.2 9.3 %shard_map.231 = (bf16[768,1024]{1,0:T(8,128)(2,1)}, bf16[4,256,256]{2,1,0:T(8,128)(2,1)}, f32[8,1024]{1,0:T(8,128)}) custom-call(bf16[4,1024,256]{2,1,0:T(8,128)(2,1)} %multiply_convert_fusion.x.refs_0_, bf16[1024,768]{1,0:T(8,128)(2,1)} %bitcast.109, f32[1,768]{1,0:T(1,128)} %get-tuple-element.127.bias, f32[8,512]{1,0:T(8,128)} %get-tuple-element.131.cosine, ...), custom_call_target="tpu_custom_call" | custom-call | flops 2147483648 | bytes 3670016 | tf_op jit(solution)/shard_map/pallas_call | solution.py:587
  180.6 4.8 shard_map.232
  185.3 8.6 %shard_map.233 = (bf16[4,1024,256]{2,1,0:T(8,128)(2,1)}, bf16[4,1024,256]{2,1,0:T(8,128)(2,1)}) custom-call(bf16[4,1024,256]{2,1,0:T(8,128)(2,1)} %multiply_convert_fusion.x.refs_0_, bf16[1024,2304]{1,0:T(8,128)(2,1)} %bitcast.89, f32[1,1024]{1,0:T(1,128)} %get-tuple-element.125.bias), custom_call_target="tpu_custom_call" | custom-call | flops 2147483648 | bytes 8388608 | tf_op jit(solution)/shard_map/pallas_call | solution.py:610
  193.9 7.3 %shard_map.234 = bf16[4,1024,256]{2,1,0:T(8,128)(2,1)} custom-call(bf16[4,256,256]{2,1,0:T(8,128)(2,1)} %get-tuple-element.62.mixed.refs_3_, bf16[4,1024,256]{2,1,0:T(8,128)(2,1)} %get-tuple-element.65.hidden.refs_4_, bf16[1024,2304]{1,0:T(8,128)(2,1)} %bitcast.90), custom_call_target="tpu_custom_call" | custom-call | flops 2684354560 | bytes 7340032 | tf_op jit(solution)/shard_map/pallas_call | solution.py:623
  202.6 2.6 collective-permute-done.16
  209.7 11.1 %collective-permute-done.17 = bf16[1,1024,256]{2,1,0:T(8,128)(2,1)S(1)} collective-permute-done((bf16[1,1024,256]{2,1,0:T(8,128)(2,1)S(1)}, bf16[1,1024,256]{2,1,0:T(8,128)(2,1)S(1)}, u32[]{:S(2)}, u32[]{:S(2)}) %collective-permute-start.17) | collective-permute-done | bytes 524320 | tf_op jit(solution)/shard_map/ppermute | solution.py:186
  223.5 2.6 fusion.12
  227.6 11.9 %collective-permute-done.18 = bf16[1,1024,256]{2,1,0:T(8,128)(2,1)S(1)} collective-permute-done((bf16[1,1024,256]{2,1,0:T(8,128)(2,1)}, bf16[1,1024,256]{2,1,0:T(8,128)(2,1)S(1)}, u32[]{:S(2)}, u32[]{:S(2)}) %collective-permute-start.18) | collective-permute-done | bytes 524320 | tf_op jit(solution)/shard_map/ppermute | solution.py:204
  241.1 3.9 copy.38
  246.7 9.3 %shard_map.235 = (bf16[768,1024]{1,0:T(8,128)(2,1)}, bf16[4,256,256]{2,1,0:T(8,128)(2,1)}, f32[8,1024]{1,0:T(8,128)}) custom-call(bf16[4,1024,256]{2,1,0:T(8,128)(2,1)} %maximum_select_fusion.x.refs_0_, bf16[1024,3072]{1,0:T(8,128)(2,1)} %all-gather.2.cloned.1.call-done.mat.qkv_mat.up_mat, f32[1,768]{1,0:T(1,128)} %get-tuple-element.126.bias, ...), custom_call_target="tpu_custom_call" | custom-call | flops 2147483648 | bytes 3670016 | tf_op jit(solution)/shard_map/pallas_call | solution.py:587
  256.0 9.6 %shard_map.236 = (bf16[4,1024,256]{2,1,0:T(8,128)(2,1)}, bf16[4,1024,256]{2,1,0:T(8,128)(2,1)}) custom-call(bf16[4,1024,256]{2,1,0:T(8,128)(2,1)} %maximum_select_fusion.x.refs_0_, bf16[1024,3072]{1,0:T(8,128)(2,1)} %all-gather.2.cloned.1.call-done.mat.qkv_mat.up_mat, f32[1,1024]{1,0:T(1,128)} %get-tuple-element.123.bias), custom_call_target="tpu_custom_call" | custom-call | flops 2147483648 | bytes 8388608 | tf_op jit(solution)/shard_map/pallas_call | solution.py:610
  265.7 8.8 %shard_map.237 = (bf16[4,256,256]{2,1,0:T(8,128)(2,1)}, bf16[4,1024,256]{2,1,0:T(8,128)(2,1)}) custom-call(bf16[4,1024,256]{2,1,0:T(8,128)(2,1)} %bitcast.86, bf16[1024,3072]{1,0:T(8,128)(2,1)} %all-gather.2.cloned.1.call-done.mat.qkv_mat.up_mat, bf16[4,1024,256]{2,1,0:T(8,128)(2,1)} %get-tuple-element.72.slope), custom_call_target="tpu_custom_call" | custom-call | flops 2684354560 | bytes 9961472 | tf_op jit(solution)/shard_map/pallas_call | solution.py:635
  274.5 9.3 %shard_map.238.d_joined.refs_2_ = bf16[4,768,256]{2,1,0:T(8,128)(2,1)} custom-call(bf16[768,1024]{1,0:T(8,128)(2,1)} %get-tuple-element.70.qkv, f32[8,1024]{1,0:T(8,128)} %get-tuple-element.71.log_total, bf16[4,256,256]{2,1,0:T(8,128)(2,1)} %get-tuple-element.73.d_mixed, f32[8,512]{1,0:T(8,128)} %get-tuple-element.131.cosine, f32[8,512]{1,0:T(8,128)} %get-tuple-element.130.sine), custom_call_target="tpu_custom_call" | custom-call | flops 1342177280 | bytes 4718592 | tf_op jit(solution)/shard_map/pallas_call | solution.py:647
  283.8 9.2 %shard_map.239 = bf16[4,1024,256]{2,1,0:T(8,128)(2,1)} custom-call(bf16[4,768,256]{2,1,0:T(8,128)(2,1)} %shard_map.238.d_joined.refs_2_, bf16[4,1024,256]{2,1,0:T(8,128)(2,1)} %get-tuple-element.74.d_hidden.refs_3_, bf16[1024,3072]{1,0:T(8,128)(2,1)} %all-gather.2.cloned.1.call-done.mat.qkv_mat.up_mat, ...), custom_call_target="tpu_custom_call" | custom-call | flops 3758096384 | bytes 9437184 | tf_op jit(solution)/shard_map/pallas_call | solution.py:666
  294.8 2.3 collective-permute-done.20
  297.1 15.7 %shard_map.240 = bf16[8,144,3072]{2,1,0:T(8,128)(2,1)} custom-call(bf16[4,1024,256]{2,1,0:T(8,128)(2,1)} %maximum_select_fusion.x.refs_0_, bf16[4,1024,256]{2,1,0:T(8,128)(2,1)} %bitcast.87, bf16[4,768,256]{2,1,0:T(8,128)(2,1)} %shard_map.238.d_joined.refs_2_, bf16[4,1024,256]{2,1,0:T(8,128)(2,1)} %get-tuple-element.74.d_hidden.refs_3_, ...), custom_call_target="tpu_custom_call" | custom-call | flops 6442450944 | bytes 14680064 | tf_op jit(solution)/shard_map/pallas_call | solution.py:686
  312.8 7.9 %shard_map.241 = bf16[4,1024,256]{2,1,0:T(8,128)(2,1)} custom-call(bf16[4,256,256]{2,1,0:T(8,128)(2,1)} %get-tuple-element.68.refs_4_.mixed, bf16[4,1024,256]{2,1,0:T(8,128)(2,1)} %get-tuple-element.76.refs_5_.hidden, bf16[1024,3072]{1,0:T(8,128)(2,1)} %all-gather.2.cloned.1.call-done.mat.qkv_mat.up_mat), custom_call_target="tpu_custom_call" | custom-call | flops 2684354560 | bytes 7340032 | tf_op jit(solution)/shard_map/pallas_call | solution.py:623
  324.5 12.7 %collective-permute-done.25 = bf16[1,1024,256]{2,1,0:T(8,128)(2,1)S(1)} collective-permute-done((bf16[1,1024,256]{2,1,0:T(8,128)(2,1)S(1)}, bf16[1,1024,256]{2,1,0:T(8,128)(2,1)S(1)}, u32[]{:S(2)}, u32[]{:S(2)}) %collective-permute-start.25) | collective-permute-done | bytes 524320 | tf_op jit(solution)/shard_map/ppermute | solution.py:186
  339.5 11.8 %collective-permute-done.22 = bf16[1,1024,256]{2,1,0:T(8,128)(2,1)S(1)} collective-permute-done((bf16[1,1024,256]{2,1,0:T(8,128)(2,1)S(1)}, bf16[1,1024,256]{2,1,0:T(8,128)(2,1)S(1)}, u32[]{:S(2)}, u32[]{:S(2)}) %collective-permute-start.22) | collective-permute-done | bytes 524320 | tf_op jit(solution)/shard_map/ppermute | solution.py:186
  351.3 2.4 fusion.18
  355.2 11.2 %collective-permute-done.26 = bf16[1,1024,256]{2,1,0:T(8,128)(2,1)S(1)} collective-permute-done((bf16[1,1024,256]{2,1,0:T(8,128)(2,1)S(1)}, bf16[1,1024,256]{2,1,0:T(8,128)(2,1)S(1)}, u32[]{:S(2)}, u32[]{:S(2)}) %collective-permute-start.26) | collective-permute-done | bytes 524320 | tf_op jit(solution)/shard_map/ppermute | solution.py:204
  366.7 2.6 collective-permute-done.27
  370.9 8.4 %shard_map.242 = (bf16[4,256,256]{2,1,0:T(8,128)(2,1)}, bf16[4,1024,256]{2,1,0:T(8,128)(2,1)}) custom-call(bf16[4,1024,256]{2,1,0:T(8,128)(2,1)} %maximum_select_fusion.2.grad.refs_3_.refs_1_, bf16[1024,2304]{1,0:T(8,128)(2,1)} %bitcast.91, bf16[4,1024,256]{2,1,0:T(8,128)(2,1)} %get-tuple-element.79.slope), custom_call_target="tpu_custom_call" | custom-call | flops 2684354560 | bytes 9961472 | tf_op jit(solution)/shard_map/pallas_call | solution.py:635
  379.3 9.3 %shard_map.243.d_joined.refs_1_ = bf16[4,768,256]{2,1,0:T(8,128)(2,1)} custom-call(bf16[768,1024]{1,0:T(8,128)(2,1)} %get-tuple-element.77.qkv, f32[8,1024]{1,0:T(8,128)} %get-tuple-element.78.log_total, bf16[4,256,256]{2,1,0:T(8,128)(2,1)} %get-tuple-element.80.d_mixed, f32[8,512]{1,0:T(8,128)} %get-tuple-element.131.cosine, f32[8,512]{1,0:T(8,128)} %get-tuple-element.130.sine), custom_call_target="tpu_custom_call" | custom-call | flops 1342177280 | bytes 4718592 | tf_op jit(solution)/shard_map/pallas_call | solution.py:647
  388.6 9.0 %shard_map.244 = bf16[4,1024,256]{2,1,0:T(8,128)(2,1)} custom-call(bf16[4,768,256]{2,1,0:T(8,128)(2,1)} %shard_map.243.d_joined.refs_1_, bf16[4,1024,256]{2,1,0:T(8,128)(2,1)} %get-tuple-element.81.d_hidden.refs_2_, bf16[1024,768]{1,0:T(8,128)(2,1)} %bitcast.110, bf16[1024,2304]{1,0:T(8,128)(2,1)} %bitcast.92), custom_call_target="tpu_custom_call" | custom-call | flops 3758096384 | bytes 9437184 | tf_op jit(solution)/shard_map/pallas_call | solution.py:666
  397.7 2.3 constant_dynamic-slice_fusion.3
  402.6 10.0 %shard_map.250.up_piece.down_piece.piece = bf16[8,128,2304]{2,1,0:T(8,128)(2,1)} custom-call(bf16[4,1024,256]{2,1,0:T(8,128)(2,1)} %multiply_convert_fusion.x.refs_0_, bf16[4,1024,256]{2,1,0:T(8,128)(2,1)} %maximum_select_fusion.2.grad.refs_3_.refs_1_, bf16[4,1024,256]{2,1,0:T(8,128)(2,1)} %get-tuple-element.81.d_hidden.refs_2_, ...), custom_call_target="tpu_custom_call" | custom-call | flops 4831838208 | bytes 11534336 | tf_op jit(solution)/shard_map/pallas_call | solution.py:686
  419.0 9.0 %shard_map.245.up_piece.down_piece.piece = bf16[8,144,768]{2,1,0:T(8,128)(2,1)} custom-call(bf16[4,1024,256]{2,1,0:T(8,128)(2,1)} %multiply_convert_fusion.x.refs_0_, bf16[4,768,256]{2,1,0:T(8,128)(2,1)} %shard_map.243.d_joined.refs_1_, bf16[4,1024,256]{2,1,0:T(8,128)(2,1)} %get-tuple-element.81.d_hidden.refs_2_, ...), custom_call_target="tpu_custom_call" | custom-call | flops 1610612736 | bytes 5242880 | tf_op jit(solution)/shard_map/pallas_call | solution.py:686
  427.9 2.2 collective-permute-done.40.left
  430.1 9.3 %collective-permute-done.41.right = bf16[128,1152]{1,0:T(8,128)(2,1)} collective-permute-done((bf16[128,1152]{1,0:T(8,128)(2,1)S(1)}, bf16[128,1152]{1,0:T(8,128)(2,1)}, u32[]{:S(2)}, u32[]{:S(2)}) %collective-permute-start.41) | collective-permute-done | bytes 294944 | tf_op jit(solution)/shard_map/ppermute | solution.py:158
  439.5 3.7 shard_map.251
  451.0 1.8 maximum_select_fusion.5
  452.8 8.6 %collective-permute-done.32.left = bf16[144,384]{1,0:T(8,128)(2,1)S(1)} collective-permute-done((bf16[144,384]{1,0:T(8,128)(2,1)S(1)}, bf16[144,384]{1,0:T(8,128)(2,1)S(1)}, u32[]{:S(2)}, u32[]{:S(2)}) %collective-permute-start.32) | collective-permute-done | bytes 110624 | tf_op jit(solution)/shard_map/ppermute | solution.py:157
  462.7 2.6 shard_map.246
  466.1 3.4 shard_map.252
  471.5 2.4 maximum_select_fusion.7
  475.6 13.9 %collective-permute-done.35.down_in = bf16[144,768]{1,0:T(8,128)(2,1)S(1)} collective-permute-done((bf16[144,768]{1,0:T(8,128)(2,1)S(1)}, bf16[144,768]{1,0:T(8,128)(2,1)S(1)}, u32[]{:S(2)}, u32[]{:S(2)}) %collective-permute-start.35) | collective-permute-done | bytes 221216 | tf_op jit(solution)/shard_map/ppermute | solution.py:163
  490.2 2.7 shard_map.247
  496.3 3.4 shard_map.253
  502.1 16.8 %collective-permute-done.37.down_in = bf16[144,768]{1,0:T(8,128)(2,1)S(1)} collective-permute-done((bf16[144,768]{1,0:T(8,128)(2,1)S(1)}, bf16[144,768]{1,0:T(8,128)(2,1)S(1)}, u32[]{:S(2)}, u32[]{:S(2)}) %collective-permute-start.37) | collective-permute-done | bytes 221216 | tf_op jit(solution)/shard_map/ppermute | solution.py:163
  519.5 2.7 shard_map.248
  525.3 1.9 fusion
  527.2 2.4 copy.39
  531.1 2.7 shard_map.249.refs_0_
  533.8 3.3 shard_map.254.refs_1_
  537.1 2.7 fusion.1
  539.8 2.4 copy.41
  542.2 4.4 shard_map.255
  546.6 4.7 shard_map.256
  (247 shorter events, 90.0 us)
Async XLA Ops:
  7.2 29.5 %copy-start.6 = (bf16[1024,1024]{1,0:T(8,128)(2,1)S(1)}, bf16[1024,1024]{1,0:T(8,128)(2,1)}, u32[]{:S(2)}) copy-start(bf16[1024,1024]{1,0:T(8,128)(2,1)} %param.14) | copy-start | bytes 6291460
  7.2 239.5 %all-gather.2.cloned.1.call-start = ((), (), s32[]{:S(2)}) async-start(), calls=%async_computation.1 | async-start | bytes 7077888 | tf_op jit(solution)/shard_map/all_gather | solution.py:558
  13.9 8.8 %collective-permute-start = (bf16[144,768]{1,0:T(8,128)(2,1)}, bf16[144,768]{1,0:T(8,128)(2,1)S(1)}, u32[]{:S(2)}, u32[]{:S(2)}) collective-permute-start(bf16[144,768]{1,0:T(8,128)(2,1)} %get-tuple-element.59.refs_0_), channel_id=1, source_target_pairs={{8,0},{16,8},{24,16},{28,24},{20,28},{12,20},{4,12},{0,4},{9,1},{1... | collective-permute-start | bytes 663560 | tf_op jit(solution)/shard_map/ppermute | solution.py:115
  17.0 7.4 %collective-permute-start.3 = (bf16[144,768]{1,0:T(8,128)(2,1)}, bf16[144,768]{1,0:T(8,128)(2,1)S(1)}, u32[]{:S(2)}, u32[]{:S(2)}) collective-permute-start(bf16[144,768]{1,0:T(8,128)(2,1)} %get-tuple-element.59.refs_0_), channel_id=1, source_target_pairs={{0,8},{8,16},{16,24},{24,28},{28,20},{20,12},{12,4},{4,0},{1,9},{9... | collective-permute-start | bytes 663560 | tf_op jit(solution)/shard_map/ppermute | solution.py:114
  22.7 17.0 %copy-start.26 = (bf16[144,768]{1,0:T(8,128)(2,1)}, bf16[144,768]{1,0:T(8,128)(2,1)S(1)}, u32[]{:S(2)}) copy-start(bf16[144,768]{1,0:T(8,128)(2,1)S(1)} %collective-permute-done.refs_1_) | copy-start | bytes 663556
  22.7 6.6 %collective-permute-start.1 = (bf16[144,768]{1,0:T(8,128)(2,1)S(1)}, bf16[144,768]{1,0:T(8,128)(2,1)S(1)}, u32[]{:S(2)}, u32[]{:S(2)}) collective-permute-start(bf16[144,768]{1,0:T(8,128)(2,1)S(1)} %collective-permute-done.refs_1_), channel_id=1, source_target_pairs={{8,0},{16,8},{24,16},{28,24},{20,28},{12,20},{4,12},{0,4},{9,1},{1... | collective-permute-start | bytes 663560 | tf_op jit(solution)/shard_map/ppermute | solution.py:115
  24.4 15.4 %copy-start.27 = (bf16[144,768]{1,0:T(8,128)(2,1)}, bf16[144,768]{1,0:T(8,128)(2,1)S(1)}, u32[]{:S(2)}) copy-start(bf16[144,768]{1,0:T(8,128)(2,1)S(1)} %collective-permute-done.3.refs_8_) | copy-start | bytes 663556
  24.4 6.3 %collective-permute-start.4 = (bf16[144,768]{1,0:T(8,128)(2,1)S(1)}, bf16[144,768]{1,0:T(8,128)(2,1)S(1)}, u32[]{:S(2)}, u32[]{:S(2)}) collective-permute-start(bf16[144,768]{1,0:T(8,128)(2,1)S(1)} %collective-permute-done.3.refs_8_), channel_id=1, source_target_pairs={{0,8},{8,16},{16,24},{24,28},{28,20},{20,12},{12,4},{4,0},{1,9},{9... | collective-permute-start | bytes 663560 | tf_op jit(solution)/shard_map/ppermute | solution.py:114
  29.3 5.9 %collective-permute-start.2 = (bf16[144,768]{1,0:T(8,128)(2,1)S(1)}, bf16[144,768]{1,0:T(8,128)(2,1)S(1)}, u32[]{:S(2)}, u32[]{:S(2)}) collective-permute-start(bf16[144,768]{1,0:T(8,128)(2,1)S(1)} %collective-permute-done.1.refs_2_), channel_id=1, source_target_pairs={{8,0},{16,8},{24,16},{28,24},{20,28},{12,20},{4,12},{0,4},{9,1},{1... | collective-permute-start | bytes 663560 | tf_op jit(solution)/shard_map/ppermute | solution.py:115
  30.7 5.9 %collective-permute-start.5 = (bf16[144,768]{1,0:T(8,128)(2,1)S(1)}, bf16[144,768]{1,0:T(8,128)(2,1)S(1)}, u32[]{:S(2)}, u32[]{:S(2)}) collective-permute-start(bf16[144,768]{1,0:T(8,128)(2,1)S(1)} %collective-permute-done.4.refs_7_), channel_id=1, source_target_pairs={{0,8},{8,16},{16,24},{24,28},{28,20},{20,12},{12,4},{4,0},{1,9},{9... | collective-permute-start | bytes 663560 | tf_op jit(solution)/shard_map/ppermute | solution.py:114
  35.3 14.9 %copy-start.20 = (bf16[144,768]{1,0:T(8,128)(2,1)}, bf16[144,768]{1,0:T(8,128)(2,1)S(1)}, u32[]{:S(2)}) copy-start(bf16[144,768]{1,0:T(8,128)(2,1)S(1)} %collective-permute-done.2.refs_3_) | copy-start | bytes 663556
  36.7 505.6 %reduce-scatter.2.cloned.1.call-start = ((), (), s32[]{:S(2)}) async-start(), calls=%async_computation.2 | async-start | bytes 7962624 | tf_op jit(solution)/shard_map/reduce_scatter | solution.py:736
  45.0 46.6 %collective-permute-start.8 = (bf16[128,2304]{1,0:T(8,128)(2,1)S(1)}, bf16[128,2304]{1,0:T(8,128)(2,1)S(1)}, u32[]{:S(2)}, u32[]{:S(2)}) collective-permute-start(bf16[128,2304]{1,0:T(8,128)(2,1)S(1)} %copy-done.13), channel_id=1, source_target_pairs={{8,0},{16,8},{24,16},{28,24},{20,28},{12,20},{4,12},{0,4},{9,1},{1... | collective-permute-start | bytes 1769480 | tf_op jit(solution)/shard_map/ppermute | solution.py:115
  46.6 46.2 %collective-permute-start.11 = (bf16[128,2304]{1,0:T(8,128)(2,1)S(1)}, bf16[128,2304]{1,0:T(8,128)(2,1)S(1)}, u32[]{:S(2)}, u32[]{:S(2)}) collective-permute-start(bf16[128,2304]{1,0:T(8,128)(2,1)S(1)} %copy-done.13), channel_id=1, source_target_pairs={{0,8},{8,16},{16,24},{24,28},{28,20},{20,12},{12,4},{4,0},{1,9},{9... | collective-permute-start | bytes 1769480 | tf_op jit(solution)/shard_map/ppermute | solution.py:114
  49.5 25.7 %collective-permute-start.6 = (bf16[144,384]{1,0:T(8,128)(2,1)S(1)}, bf16[144,384]{1,0:T(8,128)(2,1)S(1)}, u32[]{:S(2)}, u32[]{:S(2)}) collective-permute-start(bf16[144,384]{1,0:T(8,128)(2,1)S(1)} %slice.89), channel_id=1, source_target_pairs={{0,8},{8,16},{16,24},{24,28},{28,20},{20,12},{12,4},{4,0},{1,9},{9... | collective-permute-start | bytes 331784 | tf_op jit(solution)/shard_map/ppermute | solution.py:119
  50.2 37.1 %collective-permute-start.7 = (bf16[144,384]{1,0:T(8,128)(2,1)S(1)}, bf16[144,384]{1,0:T(8,128)(2,1)S(1)}, u32[]{:S(2)}, u32[]{:S(2)}) collective-permute-start(bf16[144,384]{1,0:T(8,128)(2,1)S(1)} %slice.90), channel_id=1, source_target_pairs={{8,0},{16,8},{24,16},{28,24},{20,28},{12,20},{4,12},{0,4},{9,1},{1... | collective-permute-start | bytes 331784 | tf_op jit(solution)/shard_map/ppermute | solution.py:120
  91.6 86.9 %copy-start.14 = (bf16[128,2304]{1,0:T(8,128)(2,1)}, bf16[128,2304]{1,0:T(8,128)(2,1)S(1)}, u32[]{:S(2)}) copy-start(bf16[128,2304]{1,0:T(8,128)(2,1)S(1)} %collective-permute-done.8.refs_1_) | copy-start | bytes 1769476
  91.6 41.7 %collective-permute-start.9 = (bf16[128,2304]{1,0:T(8,128)(2,1)S(1)}, bf16[128,2304]{1,0:T(8,128)(2,1)S(1)}, u32[]{:S(2)}, u32[]{:S(2)}) collective-permute-start(bf16[128,2304]{1,0:T(8,128)(2,1)S(1)} %collective-permute-done.8.refs_1_), channel_id=1, source_target_pairs={{8,0},{16,8},{24,16},{28,24},{20,28},{12,20},{4,12},{0,4},{9,1},{1... | collective-permute-start | bytes 1769480 | tf_op jit(solution)/shard_map/ppermute | solution.py:115
  92.8 85.7 %copy-start.15 = (bf16[128,2304]{1,0:T(8,128)(2,1)}, bf16[128,2304]{1,0:T(8,128)(2,1)S(1)}, u32[]{:S(2)}) copy-start(bf16[128,2304]{1,0:T(8,128)(2,1)S(1)} %collective-permute-done.11.refs_8_) | copy-start | bytes 1769476
  92.8 40.5 %collective-permute-start.12 = (bf16[128,2304]{1,0:T(8,128)(2,1)S(1)}, bf16[128,2304]{1,0:T(8,128)(2,1)S(1)}, u32[]{:S(2)}, u32[]{:S(2)}) collective-permute-start(bf16[128,2304]{1,0:T(8,128)(2,1)S(1)} %collective-permute-done.11.refs_8_), channel_id=1, source_target_pairs={{0,8},{8,16},{16,24},{24,28},{28,20},{20,12},{12,4},{4,0},{1,9},{9... | collective-permute-start | bytes 1769480 | tf_op jit(solution)/shard_map/ppermute | solution.py:114
  133.3 45.2 %copy-start.16 = (bf16[128,2304]{1,0:T(8,128)(2,1)}, bf16[128,2304]{1,0:T(8,128)(2,1)S(1)}, u32[]{:S(2)}) copy-start(bf16[128,2304]{1,0:T(8,128)(2,1)S(1)} %collective-permute-done.9.refs_2_) | copy-start | bytes 1769476
  133.3 33.9 %collective-permute-start.10 = (bf16[128,2304]{1,0:T(8,128)(2,1)S(1)}, bf16[128,2304]{1,0:T(8,128)(2,1)S(1)}, u32[]{:S(2)}, u32[]{:S(2)}) collective-permute-start(bf16[128,2304]{1,0:T(8,128)(2,1)S(1)} %collective-permute-done.9.refs_2_), channel_id=1, source_target_pairs={{8,0},{16,8},{24,16},{28,24},{20,28},{12,20},{4,12},{0,4},{9,1},{1... | collective-permute-start | bytes 1769480 | tf_op jit(solution)/shard_map/ppermute | solution.py:115
  133.3 45.2 %copy-start.17 = (bf16[128,2304]{1,0:T(8,128)(2,1)}, bf16[128,2304]{1,0:T(8,128)(2,1)S(1)}, u32[]{:S(2)}) copy-start(bf16[128,2304]{1,0:T(8,128)(2,1)S(1)} %collective-permute-done.12.refs_7_) | copy-start | bytes 1769476
  133.3 20.5 %collective-permute-start.13 = (bf16[128,2304]{1,0:T(8,128)(2,1)S(1)}, bf16[128,2304]{1,0:T(8,128)(2,1)S(1)}, u32[]{:S(2)}, u32[]{:S(2)}) collective-permute-start(bf16[128,2304]{1,0:T(8,128)(2,1)S(1)} %collective-permute-done.12.refs_7_), channel_id=1, source_target_pairs={{0,8},{8,16},{16,24},{24,28},{28,20},{20,12},{12,4},{4,0},{1,9},{9... | collective-permute-start | bytes 1769480 | tf_op jit(solution)/shard_map/ppermute | solution.py:114
  153.8 24.7 %copy-start.11 = (bf16[128,2304]{1,0:T(8,128)(2,1)}, bf16[128,2304]{1,0:T(8,128)(2,1)S(1)}, u32[]{:S(2)}) copy-start(bf16[128,2304]{1,0:T(8,128)(2,1)S(1)} %collective-permute-done.13.refs_6_) | copy-start | bytes 1769476
  153.8 25.3 %collective-permute-start.14 = (bf16[128,1152]{1,0:T(8,128)(2,1)S(1)}, bf16[128,1152]{1,0:T(8,128)(2,1)S(1)}, u32[]{:S(2)}, u32[]{:S(2)}) collective-permute-start(bf16[128,1152]{1,0:T(8,128)(2,1)S(1)} %slice.94), channel_id=1, source_target_pairs={{0,8},{8,16},{16,24},{24,28},{28,20},{20,12},{12,4},{4,0},{1,9},{9... | collective-permute-start | bytes 884744 | tf_op jit(solution)/shard_map/ppermute | solution.py:119
  167.2 11.9 %collective-permute-start.15 = (bf16[128,1152]{1,0:T(8,128)(2,1)S(1)}, bf16[128,1152]{1,0:T(8,128)(2,1)S(1)}, u32[]{:S(2)}, u32[]{:S(2)}) collective-permute-start(bf16[128,1152]{1,0:T(8,128)(2,1)S(1)} %slice.95), channel_id=1, source_target_pairs={{8,0},{16,8},{24,16},{28,24},{20,28},{12,20},{4,12},{0,4},{9,1},{1... | collective-permute-start | bytes 884744 | tf_op jit(solution)/shard_map/ppermute | solution.py:120
  202.5 2.7 collective-permute-start.16
  206.8 14.0 %collective-permute-start.17 = (bf16[1,1024,256]{2,1,0:T(8,128)(2,1)S(1)}, bf16[1,1024,256]{2,1,0:T(8,128)(2,1)S(1)}, u32[]{:S(2)}, u32[]{:S(2)}) collective-permute-start(bf16[1,1024,256]{2,1,0:T(8,128)(2,1)S(1)} %dynamic-slice_convert_fusion.3), channel_id=1, source_target_pairs={{0,2},{1,3},{2,0},{3,1},{4,6},{5,7},{6,4},{7,5},{8,10},{9,11},{10,... | collective-permute-start | bytes 1572872 | tf_op jit(solution)/shard_map/ppermute | solution.py:186
  226.2 13.3 %collective-permute-start.18 = (bf16[1,1024,256]{2,1,0:T(8,128)(2,1)}, bf16[1,1024,256]{2,1,0:T(8,128)(2,1)S(1)}, u32[]{:S(2)}, u32[]{:S(2)}) collective-permute-start(bf16[1,1024,256]{2,1,0:T(8,128)(2,1)} %get-tuple-element.108), channel_id=1, source_target_pairs={{0,2},{1,3},{2,0},{3,1},{4,6},{5,7},{6,4},{7,5},{8,10},{9,11},{10,... | collective-permute-start | bytes 1572872 | tf_op jit(solution)/shard_map/ppermute | solution.py:204
  241.1 4.0 collective-permute-start.19
  294.2 2.8 collective-permute-start.20
  322.2 15.3 %collective-permute-start.21 = (bf16[2,1024,256]{2,1,0:T(8,128)(2,1)S(1)}, bf16[2,1024,256]{2,1,0:T(8,128)(2,1)S(1)}, u32[]{:S(2)}, u32[]{:S(2)}) collective-permute-start(bf16[2,1024,256]{2,1,0:T(8,128)(2,1)S(1)} %constant_dynamic-slice_fusion.4), channel_id=1, source_target_pairs={{0,1},{1,0},{2,3},{3,2},{4,5},{5,4},{6,7},{7,6},{8,9},{9,8},{10,11... | collective-permute-start | bytes 3145736 | tf_op jit(solution)/shard_map/ppermute | solution.py:186
  323.0 14.3 %collective-permute-start.25 = (bf16[1,1024,256]{2,1,0:T(8,128)(2,1)S(1)}, bf16[1,1024,256]{2,1,0:T(8,128)(2,1)S(1)}, u32[]{:S(2)}, u32[]{:S(2)}) collective-permute-start(bf16[1,1024,256]{2,1,0:T(8,128)(2,1)S(1)} %dynamic-slice_convert_fusion.1), channel_id=1, source_target_pairs={{0,2},{1,3},{2,0},{3,1},{4,6},{5,7},{6,4},{7,5},{8,10},{9,11},{10,... | collective-permute-start | bytes 1572872 | tf_op jit(solution)/shard_map/ppermute | solution.py:186
  337.8 13.5 %collective-permute-start.22 = (bf16[1,1024,256]{2,1,0:T(8,128)(2,1)S(1)}, bf16[1,1024,256]{2,1,0:T(8,128)(2,1)S(1)}, u32[]{:S(2)}, u32[]{:S(2)}) collective-permute-start(bf16[1,1024,256]{2,1,0:T(8,128)(2,1)S(1)} %dynamic-slice_convert_fusion.2), channel_id=1, source_target_pairs={{0,2},{1,3},{2,0},{3,1},{4,6},{5,7},{6,4},{7,5},{8,10},{9,11},{10,... | collective-permute-start | bytes 1572872 | tf_op jit(solution)/shard_map/ppermute | solution.py:186
  353.7 12.7 %collective-permute-start.26 = (bf16[1,1024,256]{2,1,0:T(8,128)(2,1)S(1)}, bf16[1,1024,256]{2,1,0:T(8,128)(2,1)S(1)}, u32[]{:S(2)}, u32[]{:S(2)}) collective-permute-start(bf16[1,1024,256]{2,1,0:T(8,128)(2,1)S(1)} %get-tuple-element.106), channel_id=1, source_target_pairs={{0,2},{1,3},{2,0},{3,1},{4,6},{5,7},{6,4},{7,5},{8,10},{9,11},{10,... | collective-permute-start | bytes 1572872 | tf_op jit(solution)/shard_map/ppermute | solution.py:204
  366.6 2.7 collective-permute-start.27
  399.9 13.8 %collective-permute-start.28 = (bf16[2,1024,256]{2,1,0:T(8,128)(2,1)}, bf16[2,1024,256]{2,1,0:T(8,128)(2,1)S(1)}, u32[]{:S(2)}, u32[]{:S(2)}) collective-permute-start(bf16[2,1024,256]{2,1,0:T(8,128)(2,1)} %constant_dynamic-slice_fusion.3), channel_id=1, source_target_pairs={{0,1},{1,0},{2,3},{3,2},{4,5},{5,4},{6,7},{7,6},{8,9},{9,8},{10,11... | collective-permute-start | bytes 3145736 | tf_op jit(solution)/shard_map/ppermute | solution.py:186
  414.8 30.6 %collective-permute-start.29 = (bf16[1,1024,256]{2,1,0:T(8,128)(2,1)}, bf16[1,1024,256]{2,1,0:T(8,128)(2,1)S(1)}, u32[]{:S(2)}, u32[]{:S(2)}) collective-permute-start(bf16[1,1024,256]{2,1,0:T(8,128)(2,1)} %dynamic-slice_convert_fusion), channel_id=1, source_target_pairs={{0,2},{1,3},{2,0},{3,1},{4,6},{5,7},{6,4},{7,5},{8,10},{9,11},{10,... | collective-permute-start | bytes 1572872 | tf_op jit(solution)/shard_map/ppermute | solution.py:186
  416.3 13.8 %collective-permute-start.40 = (bf16[128,1152]{1,0:T(8,128)(2,1)S(1)}, bf16[128,1152]{1,0:T(8,128)(2,1)S(1)}, u32[]{:S(2)}, u32[]{:S(2)}) collective-permute-start(bf16[128,1152]{1,0:T(8,128)(2,1)S(1)} %get-tuple-element.115), channel_id=1, source_target_pairs={{0,8},{8,16},{16,24},{24,28},{28,20},{20,12},{12,4},{4,0},{1,9},{9... | collective-permute-start | bytes 884744 | tf_op jit(solution)/shard_map/ppermute | solution.py:157
  416.6 22.8 %collective-permute-start.41 = (bf16[128,1152]{1,0:T(8,128)(2,1)S(1)}, bf16[128,1152]{1,0:T(8,128)(2,1)}, u32[]{:S(2)}, u32[]{:S(2)}) collective-permute-start(bf16[128,1152]{1,0:T(8,128)(2,1)S(1)} %get-tuple-element.114), channel_id=1, source_target_pairs={{8,0},{16,8},{24,16},{28,24},{20,28},{12,20},{4,12},{0,4},{9,1},{1... | collective-permute-start | bytes 884744 | tf_op jit(solution)/shard_map/ppermute | solution.py:158
  418.4 32.2 %collective-permute-start.23 = (bf16[1,1024,256]{2,1,0:T(8,128)(2,1)}, bf16[1,1024,256]{2,1,0:T(8,128)(2,1)}, u32[]{:S(2)}, u32[]{:S(2)}) collective-permute-start(bf16[1,1024,256]{2,1,0:T(8,128)(2,1)} %get-tuple-element.113), channel_id=1, source_target_pairs={{0,2},{1,3},{2,0},{3,1},{4,6},{5,7},{6,4},{7,5},{8,10},{9,11},{10,... | collective-permute-start | bytes 1572872 | tf_op jit(solution)/shard_map/ppermute | solution.py:204
  443.2 22.9 %collective-permute-start.42 = (bf16[128,2304]{1,0:T(8,128)(2,1)}, bf16[128,2304]{1,0:T(8,128)(2,1)}, u32[]{:S(2)}, u32[]{:S(2)}) collective-permute-start(bf16[128,2304]{1,0:T(8,128)(2,1)} %get-tuple-element.88), channel_id=1, source_target_pairs={{0,8},{8,16},{16,24},{24,28},{28,20},{20,12},{12,4},{4,0},{1,9},{9... | collective-permute-start | bytes 1769480 | tf_op jit(solution)/shard_map/ppermute | solution.py:162
  444.7 21.4 %collective-permute-start.43 = (bf16[128,2304]{1,0:T(8,128)(2,1)}, bf16[128,2304]{1,0:T(8,128)(2,1)}, u32[]{:S(2)}, u32[]{:S(2)}) collective-permute-start(bf16[128,2304]{1,0:T(8,128)(2,1)} %get-tuple-element.89), channel_id=1, source_target_pairs={{8,0},{16,8},{24,16},{28,24},{20,28},{12,20},{4,12},{0,4},{9,1},{1... | collective-permute-start | bytes 1769480 | tf_op jit(solution)/shard_map/ppermute | solution.py:163
  447.0 24.5 %collective-permute-start.30 = (bf16[1,1024,256]{2,1,0:T(8,128)(2,1)}, bf16[1,1024,256]{2,1,0:T(8,128)(2,1)S(1)}, u32[]{:S(2)}, u32[]{:S(2)}) collective-permute-start(bf16[1,1024,256]{2,1,0:T(8,128)(2,1)} %fusion.11), channel_id=1, source_target_pairs={{0,2},{1,3},{2,0},{3,1},{4,6},{5,7},{6,4},{7,5},{8,10},{9,11},{10,... | collective-permute-start | bytes 1572872 | tf_op jit(solution)/shard_map/ppermute | solution.py:204
  448.8 12.6 %collective-permute-start.32 = (bf16[144,384]{1,0:T(8,128)(2,1)S(1)}, bf16[144,384]{1,0:T(8,128)(2,1)S(1)}, u32[]{:S(2)}, u32[]{:S(2)}) collective-permute-start(bf16[144,384]{1,0:T(8,128)(2,1)S(1)} %get-tuple-element.117), channel_id=1, source_target_pairs={{0,8},{8,16},{16,24},{24,28},{28,20},{20,12},{12,4},{4,0},{1,9},{9... | collective-permute-start | bytes 331784 | tf_op jit(solution)/shard_map/ppermute | solution.py:157
  450.6 11.5 %collective-permute-start.33 = (bf16[144,384]{1,0:T(8,128)(2,1)S(1)}, bf16[144,384]{1,0:T(8,128)(2,1)S(1)}, u32[]{:S(2)}, u32[]{:S(2)}) collective-permute-start(bf16[144,384]{1,0:T(8,128)(2,1)S(1)} %get-tuple-element.116), channel_id=1, source_target_pairs={{8,0},{16,8},{24,16},{28,24},{20,28},{12,20},{4,12},{0,4},{9,1},{1... | collective-permute-start | bytes 331784 | tf_op jit(solution)/shard_map/ppermute | solution.py:158
  461.4 62.5 %collective-permute-start.24 = (bf16[2,1024,256]{2,1,0:T(8,128)(2,1)S(1)}, bf16[2,1024,256]{2,1,0:T(8,128)(2,1)S(1)}, u32[]{:S(2)}, u32[]{:S(2)}) collective-permute-start(bf16[2,1024,256]{2,1,0:T(8,128)(2,1)S(1)} %maximum_select_fusion.5), channel_id=1, source_target_pairs={{0,1},{1,0},{2,3},{3,2},{4,5},{5,4},{6,7},{7,6},{8,9},{9,8},{10,11... | collective-permute-start | bytes 3145736 | tf_op jit(solution)/shard_map/ppermute | solution.py:204
  465.3 8.6 %collective-permute-start.34 = (bf16[144,768]{1,0:T(8,128)(2,1)}, bf16[144,768]{1,0:T(8,128)(2,1)S(1)}, u32[]{:S(2)}, u32[]{:S(2)}) collective-permute-start(bf16[144,768]{1,0:T(8,128)(2,1)} %get-tuple-element.82), channel_id=1, source_target_pairs={{0,8},{8,16},{16,24},{24,28},{28,20},{20,12},{12,4},{4,0},{1,9},{9... | collective-permute-start | bytes 663560 | tf_op jit(solution)/shard_map/ppermute | solution.py:162
  469.5 25.2 %collective-permute-start.44 = (bf16[128,2304]{1,0:T(8,128)(2,1)}, bf16[128,2304]{1,0:T(8,128)(2,1)S(1)}, u32[]{:S(2)}, u32[]{:S(2)}) collective-permute-start(bf16[128,2304]{1,0:T(8,128)(2,1)} %get-tuple-element.90), channel_id=1, source_target_pairs={{0,8},{8,16},{16,24},{24,28},{28,20},{20,12},{12,4},{4,0},{1,9},{9... | collective-permute-start | bytes 1769480 | tf_op jit(solution)/shard_map/ppermute | solution.py:162
  470.9 23.8 %collective-permute-start.45 = (bf16[128,2304]{1,0:T(8,128)(2,1)}, bf16[128,2304]{1,0:T(8,128)(2,1)S(1)}, u32[]{:S(2)}, u32[]{:S(2)}) collective-permute-start(bf16[128,2304]{1,0:T(8,128)(2,1)} %get-tuple-element.91), channel_id=1, source_target_pairs={{8,0},{16,8},{24,16},{28,24},{20,28},{12,20},{4,12},{0,4},{9,1},{1... | collective-permute-start | bytes 1769480 | tf_op jit(solution)/shard_map/ppermute | solution.py:163
  473.9 63.2 %collective-permute-start.31 = (bf16[2,1024,256]{2,1,0:T(8,128)(2,1)}, bf16[2,1024,256]{2,1,0:T(8,128)(2,1)}, u32[]{:S(2)}, u32[]{:S(2)}) collective-permute-start(bf16[2,1024,256]{2,1,0:T(8,128)(2,1)} %maximum_select_fusion.7), channel_id=1, source_target_pairs={{0,1},{1,0},{2,3},{3,2},{4,5},{5,4},{6,7},{7,6},{8,9},{9,8},{10,11... | collective-permute-start | bytes 3145736 | tf_op jit(solution)/shard_map/ppermute | solution.py:204
  473.9 15.6 %copy-start.30 = (bf16[144,768]{1,0:T(8,128)(2,1)}, bf16[144,768]{1,0:T(8,128)(2,1)S(1)}, u32[]{:S(2)}) copy-start(bf16[144,768]{1,0:T(8,128)(2,1)S(1)} %collective-permute-done.34.up_in) | copy-start | bytes 663556
  473.9 15.6 %collective-permute-start.35 = (bf16[144,768]{1,0:T(8,128)(2,1)S(1)}, bf16[144,768]{1,0:T(8,128)(2,1)S(1)}, u32[]{:S(2)}, u32[]{:S(2)}) collective-permute-start(bf16[144,768]{1,0:T(8,128)(2,1)S(1)} %copy-done.40), channel_id=1, source_target_pairs={{8,0},{16,8},{24,16},{28,24},{20,28},{12,20},{4,12},{0,4},{9,1},{1... | collective-permute-start | bytes 663560 | tf_op jit(solution)/shard_map/ppermute | solution.py:163
  492.9 8.8 %collective-permute-start.36 = (bf16[144,768]{1,0:T(8,128)(2,1)}, bf16[144,768]{1,0:T(8,128)(2,1)S(1)}, u32[]{:S(2)}, u32[]{:S(2)}) collective-permute-start(bf16[144,768]{1,0:T(8,128)(2,1)} %get-tuple-element.84), channel_id=1, source_target_pairs={{0,8},{8,16},{16,24},{24,28},{28,20},{20,12},{12,4},{4,0},{1,9},{9... | collective-permute-start | bytes 663560 | tf_op jit(solution)/shard_map/ppermute | solution.py:162
  499.7 34.1 %collective-permute-start.46 = (bf16[128,2304]{1,0:T(8,128)(2,1)}, bf16[128,2304]{1,0:T(8,128)(2,1)}, u32[]{:S(2)}, u32[]{:S(2)}) collective-permute-start(bf16[128,2304]{1,0:T(8,128)(2,1)} %get-tuple-element.92), channel_id=1, source_target_pairs={{0,8},{8,16},{16,24},{24,28},{28,20},{20,12},{12,4},{4,0},{1,9},{9... | collective-permute-start | bytes 1769480 | tf_op jit(solution)/shard_map/ppermute | solution.py:162
  501.4 32.5 %collective-permute-start.47 = (bf16[128,2304]{1,0:T(8,128)(2,1)}, bf16[128,2304]{1,0:T(8,128)(2,1)}, u32[]{:S(2)}, u32[]{:S(2)}) collective-permute-start(bf16[128,2304]{1,0:T(8,128)(2,1)} %get-tuple-element.93), channel_id=1, source_target_pairs={{8,0},{16,8},{24,16},{28,24},{20,28},{12,20},{4,12},{0,4},{9,1},{1... | collective-permute-start | bytes 1769480 | tf_op jit(solution)/shard_map/ppermute | solution.py:163
  501.7 17.1 %copy-start.31 = (bf16[144,768]{1,0:T(8,128)(2,1)}, bf16[144,768]{1,0:T(8,128)(2,1)S(1)}, u32[]{:S(2)}) copy-start(bf16[144,768]{1,0:T(8,128)(2,1)S(1)} %collective-permute-done.36.up_in) | copy-start | bytes 663556
  501.7 17.1 %collective-permute-start.37 = (bf16[144,768]{1,0:T(8,128)(2,1)S(1)}, bf16[144,768]{1,0:T(8,128)(2,1)S(1)}, u32[]{:S(2)}, u32[]{:S(2)}) collective-permute-start(bf16[144,768]{1,0:T(8,128)(2,1)S(1)} %copy-done.41), channel_id=1, source_target_pairs={{8,0},{16,8},{24,16},{28,24},{20,28},{12,20},{4,12},{0,4},{9,1},{1... | collective-permute-start | bytes 663560 | tf_op jit(solution)/shard_map/ppermute | solution.py:163
  522.3 7.3 %collective-permute-start.38 = (bf16[144,768]{1,0:T(8,128)(2,1)}, bf16[144,768]{1,0:T(8,128)(2,1)S(1)}, u32[]{:S(2)}, u32[]{:S(2)}) collective-permute-start(bf16[144,768]{1,0:T(8,128)(2,1)} %get-tuple-element.86), channel_id=1, source_target_pairs={{0,8},{8,16},{16,24},{24,28},{28,20},{20,12},{12,4},{4,0},{1,9},{9... | collective-permute-start | bytes 663560 | tf_op jit(solution)/shard_map/ppermute | solution.py:162
  524.9 6.2 %collective-permute-start.39 = (bf16[144,768]{1,0:T(8,128)(2,1)}, bf16[144,768]{1,0:T(8,128)(2,1)}, u32[]{:S(2)}, u32[]{:S(2)}) collective-permute-start(bf16[144,768]{1,0:T(8,128)(2,1)} %get-tuple-element.87), channel_id=1, source_target_pairs={{8,0},{16,8},{24,16},{28,24},{20,28},{12,20},{4,12},{0,4},{9,1},{1... | collective-permute-start | bytes 663560 | tf_op jit(solution)/shard_map/ppermute | solution.py:163
  551.3 4.7 collective-permute-start.50
  551.3 4.7 collective-permute-start.49
  553.0 3.0 collective-permute-start.48
  (32 other events, 153.9 us)
Sparse Core Ops, SparseCore 0:
  36.8 129.9 all-gather.1
  312.9 135.0 reduce-scatter.1
where the time goes:
time: 571 us; the launch traced here: 565 us
  waiting for transfers between devices  227 us (40%)
  Pallas kernels  185 us (32%)
  starting transfers between devices  60.9 us (11%)
  local copies, waits for them, and re-layouts  38.3 us (7%)
  other arithmetic  36.6 us (6%)
  between operations  16.8 us (3%)
    ppermute x6, waiting for transfers between devices, gather(): down = lax.ppermute(down, 'shard', self.back)  54.3 us
    ppermute x8, waiting for transfers between devices, tensor_scatter(): got = lax.ppermute(give.astype(BF), 'tensor', partner(bit))  40.6 us
    pallas_call x3, Pallas kernels, grads_of(): call(functools.partial(grad_kernel, pairs, sums), shape((count, high, col...  34.6 us
    ppermute x6, waiting for transfers between devices, scatter(): down = lax.ppermute(down, 'shard', self.back)  32.3 us
    ppermute x8, waiting for transfers between devices, tensor_gather(): got = lax.ppermute(part, 'tensor', partner(bit))  25.7 us
    pallas_call x8, Pallas kernels, add(): pl.pallas_call(kernel, out_shape=outs, grid_spec=pltpu.PrefetchScalarGrid...  24.6 us
    ppermute x2, waiting for transfers between devices, gather(): pieces[far] = lax.ppermute(up[:, :half], 'shard', self.ahead)  22.3 us
    ppermute x6, waiting for transfers between devices, gather(): up = lax.ppermute(up, 'shard', self.ahead)  19.2 us
  transfers between devices with their start and end apart: 53, of which 24 were waited for; matrix products, arithmetic and copies ran while one was open for 11% of the time, Pallas kernels for 20%

commit v1 on v0

--- a/solution.py
+++ b/solution.py
@@ -103,19 +103,23 @@
         self.owner = jnp.array(self.order, jnp.int32)[(place + steps) % self.count]
         self.me = me
 
-    def gather(self, part, rows, gate=None):
+    def gather(self, part, rows, gate=None, holds=None):
         count, cols = self.count, part.shape[1]
         half, far = cols // 2, self.count // 2
         if gate is not None:
-            part = after(part, gate)
+            part = after(part, *gate)
         up = down = part
         pieces = [part] + [None] * count
+        holds = holds or {}
+        gate = []
         for step in range(1, far):
+            if step in holds:
+                up, down = lax.optimization_barrier((up, down, holds[step]))[:2]
             up = lax.ppermute(up, "shard", self.ahead)
             down = lax.ppermute(down, "shard", self.back)
             pieces[count + 1 - step] = up
             pieces[step] = down
-        gate = (up, down)
+            gate.append((up, down))
         pieces[far] = lax.ppermute(up[:, :half], "shard", self.ahead)
         pieces[far + 1] = lax.ppermute(down[:, half:], "shard", self.back)
         outs = [shape((count, rows, cols))]
@@ -130,11 +134,11 @@
         )(self.owner, *pieces)
         return [result[0].reshape(count * rows, cols)] + list(result[1:]), gate
 
-    def scatter(self, total):
+    def scatter(self, total, hold=None):
         count, rows, cols = total.shape
         half, far = cols // 2, count // 2
 
-        def add(kernel, ups, chosen, outs):
+        def add(kernel, ups, chosen, outs, total=total):
             def place(which):
                 return pl.BlockSpec((1, rows, cols), lambda i, own: (own[which], 0, 0))
 
@@ -163,7 +167,9 @@
             down = lax.ppermute(down, "shard", self.back)
             if step > 1:
                 up, down = add(add_kernel, (up, down), (step - 1, count - step + 1), pair)
-        return add(add_last_kernel, (up, down), (0,), [shape((rows, cols), F32)])[0]
+        if hold is not None:
+            total = after(total, hold)
+        return add(add_last_kernel, (up, down), (0,), [shape((rows, cols), F32)], total)[0]
 
 
 def partner(bit):
@@ -184,7 +190,7 @@
         keep = lax.dynamic_slice_in_dim(part, side * rows, rows, 0)
         give = lax.dynamic_slice_in_dim(part, (1 - side) * rows, rows, 0)
         got = lax.ppermute(give.astype(BF), "tensor", partner(bit))
-        first = got if first is None else first
+        first = give
         part = keep.astype(F32) + got.astype(F32)
     return part[0], first
 
@@ -264,12 +270,13 @@
         for value in (high, total - high):
             for at in range(0, total.shape[1], qkv_cols):
                 tail.append(value[:, at : at + qkv_cols])
-        first, second, at = (outs[0], outs[1], 0) if layer == 0 else (outs[2], outs[2], qkv_cols)
-        first[:rows, :qkv_cols] = scaled[0]
-        second[:, at : at + up_cols] = scaled[1]
-        at += up_cols
-        second[:, at : at + mix_cols] = w_dense[layer].astype(F32).T.astype(BF)
-        second[:, at + mix_cols :] = w_down[layer].astype(F32).T.astype(BF)
+        first, second, third = (0, 1, 1) if layer == 0 else (2, 2, 3)
+        outs[first][:rows, :qkv_cols] = scaled[0]
+        at = 0 if layer == 0 else qkv_cols
+        outs[second][:, at : at + up_cols] = scaled[1]
+        at = up_cols if layer == 0 else 0
+        outs[third][:, at : at + mix_cols] = w_dense[layer].astype(F32).T.astype(BF)
+        outs[third][:, at + mix_cols :] = w_down[layer].astype(F32).T.astype(BF)
     outs[0][rows:, :] = jnp.concatenate(tail, axis=0).astype(BF)
 
 
@@ -550,17 +557,13 @@
         [
             shape((rows + EXTRA, qkv_cols)),
             shape((rows, rest_cols)),
-            shape((rows, in_cols + out_cols)),
+            shape((rows, in_cols)),
+            shape((rows, out_cols)),
         ],
         moved=8 * rows * (in_cols + out_cols),
     )(norms, own, w_qkv, w_fc1, w_dense, w_fc2)
-    (qkv_0, tail), gate = ring.gather(packed[0], rows)
-    all_1 = lax.all_gather(after(packed[2], gate), "shard", axis=0, tiled=True)
-    (rest_0,), gate = ring.gather(packed[1], rows, gate)
-    mats = [
-        ((qkv_0, 0), (rest_0, 0), (rest_0, ff_cols)),
-        ((all_1, 0), (all_1, qkv_cols), (all_1, in_cols)),
-    ]
+    (qkv_0, tail), hops = ring.gather(packed[0], rows)
+    mats = [[(qkv_0, 0)], []]
     tail = tail.reshape(LAYERS, 2, small)
     biases = tail[:, 0] + tail[:, 1]
 
@@ -709,9 +712,17 @@
     resid_0 = tensor_own(token_blocks)
     own_normed_0, factor_0 = normalize(resid_0)
     normed_0 = normalize(token_blocks)[0].astype(BF)
+    far = count // 2
+    last = far - 1
     qkv_rows_0, mixed_0, log_0 = attend(normed_0, 0)
+    (rest_0,), hops = ring.gather(packed[1], rows, hops[-1], {last: mixed_0})
+    mats[0] += [(rest_0, 0), (rest_0, ff_cols)]
     hidden_0, slope_0 = widen(normed_0, 0)
-    branch, _ = tensor_scatter(branch_of(mixed_0, hidden_0, 0))
+    partial = branch_of(mixed_0, hidden_0, 0)
+    (in_1,), hops = ring.gather(packed[2], rows, hops[max(last - 2, 0)], {last: partial})
+    (out_1,), hops = ring.gather(packed[3], rows, hops[max(last - 2, 0)])
+    mats[1] += [(in_1, 0), (in_1, qkv_cols), (out_1, 0)]
+    branch, _ = tensor_scatter(partial)
     resid_1 = resid_0 + branch + biases[0, in_cols : in_cols + model][:, None]
     own_normed_1, factor_1 = normalize(resid_1)
     normed_1 = tensor_gather(own_normed_1.astype(BF))
@@ -735,21 +746,20 @@
     )
     sum_1 = lax.psum_scatter(total_1, "shard", scatter_dimension=0, tiled=True)[0]
     grad_1 = grad_step(tensor_own(grad_low_2).astype(F32), shaped, own_normed_1, factor_1)
-    grad_low_1 = tensor_gather(grad_1.astype(BF))
-
-    branch, _ = tensor_scatter(branch_of(mixed_1, after(hidden_1, total_1), 1))
+    own_low_1 = grad_1.astype(BF)
+    grad_low_1 = tensor_gather(own_low_1)
+
+    branch, _ = tensor_scatter(branch_of(mixed_1, after(hidden_1, total_1, own_low_1), 1))
     resid_2 = resid_1 + branch + biases[1, in_cols : in_cols + model][:, None]
     output = tensor_gather(resid_2.astype(BF))
 
     d_mixed, d_hidden = narrow(grad_low_1, slope_0, 0)
-    rest_sum = ring.scatter(
-        grads_of(((0, 2), (1, 3), (1, 4)), (), normed_0, grad_low_1, d_hidden, mixed_0, hidden_0)
+    rest_grads = grads_of(
+        ((0, 2), (1, 3), (1, 4)), (), normed_0, grad_low_1, d_hidden, mixed_0, hidden_0
     )
-    d_joined = attend_back(qkv_rows_0, log_0, d_mixed)
-    qkv_sum = ring.scatter(
-        grads_of(((0, 1),), (1, 2, 3), normed_0, d_joined, d_hidden, grad_low_1)
-    )
-    shaped, _ = tensor_scatter(shaped_of(d_joined, d_hidden, 0))
+    d_joined = attend_back(qkv_rows_0, log_0, after(d_mixed, rest_grads))
+    qkv_grads = grads_of(((0, 1),), (1, 2, 3), normed_0, d_joined, d_hidden, grad_low_1)
+    shaped, _ = tensor_scatter(shaped_of(after(d_joined, qkv_grads), d_hidden, 0))
     grad_0 = grad_step(grad_1, shaped, own_normed_0, factor_0)
     grad_low_0 = tensor_gather(grad_0.astype(BF))
 
@@ -775,6 +785,8 @@
         )(norms, w_qkv, w_fc1, *parts, *kept)
 
     kept = finish(1, (sum_1,), ())
+    rest_sum = ring.scatter(rest_grads)
+    qkv_sum = ring.scatter(qkv_grads, kept[4])
     d_qkv, d_up, d_dense, d_down, d_norm, sums = finish(0, (qkv_sum, rest_sum), kept)
     d_norm = tensor_small_sum(d_norm)
     sums = sums[:, 0]

time: 571 us -> 541 us (0.947)
  waiting for transfers between devices: 227 us -> 180 us
  local copies, waits for them, and re-layouts: 38.3 us -> 45.2 us
    ppermute x6 -> x12, waiting for transfers between devices: 54.3 us -> 21.4 us  [gather(): down = lax.ppermute(down, 'shard', self.back)]
    ppermute x6 -> x12, waiting for transfers between devices: 19.2 us -> 41.8 us  [gather(): up = lax.ppermute(up, 'shard', self.ahead)]
    ppermute x2 -> x4, waiting for transfers between devices: 22.3 us -> 3.61 us  [gather(): pieces[far] = lax.ppermute(up[:, :half], 'shard', self.ahead)]
    ppermute x6 -> x12, starting transfers between devices: 8.91 us -> 21 us  [gather(): down = lax.ppermute(down, 'shard', self.back)]
    ppermute x2 -> x4, starting transfers between devices: 13.5 us -> 1.68 us  [gather(): pieces[far] = lax.ppermute(up[:, :half], 'shard', self.ahead)]
    ppermute x2 -> x4, waiting for transfers between devices: 12.1 us -> 1.19 us  [gather(): pieces[far + 1] = lax.ppermute(down[:, half:], 'shard', self.back)]
    ppermute x8, waiting for transfers between devices: 25.7 us -> 15.1 us  [tensor_gather(): got = lax.ppermute(part, 'tensor', partner(bit))]
    pallas_call x2 -> x4, Pallas kernels: 7.61 us -> 15 us  [gather(): call(functools.partial(assemble_kernel, count, rows), outs, moved=4 * cou...]
  transfers between devices with their start and end apart: 53 -> 68, of which waited for: 24 -> 29; matrix products, arithmetic and copies ran while one was open for 11% -> 11% of each run, Pallas kernels for 20% -> 19%
where the time goes in v1:
time: 541 us; the launch traced here: 531 us
  Pallas kernels  189 us (35%)
  waiting for transfers between devices  180 us (33%)
  starting transfers between devices  61.6 us (11%)
  local copies, waits for them, and re-layouts  45.2 us (8%)
  other arithmetic  37.9 us (7%)
  between operations  16.8 us (3%)
    ppermute x12, waiting for transfers between devices, gather(): up = lax.ppermute(up, 'shard', self.ahead)  41.8 us
    ppermute x8, waiting for transfers between devices, tensor_scatter(): got = lax.ppermute(give.astype(BF), 'tensor', partner(bit))  40.6 us
    pallas_call x3, Pallas kernels, grads_of(): call(functools.partial(grad_kernel, pairs, sums), shape((count, high, col...  34.7 us
    ppermute x6, waiting for transfers between devices, scatter(): down = lax.ppermute(down, 'shard', self.back)  31.3 us
    pallas_call x8, Pallas kernels, add(): pl.pallas_call(kernel, out_shape=outs, grid_spec=pltpu.PrefetchScalarGrid...  24.6 us
    ppermute x12, waiting for transfers between devices, gather(): down = lax.ppermute(down, 'shard', self.back)  21.4 us
    ppermute x12, starting transfers between devices, gather(): down = lax.ppermute(down, 'shard', self.back)  21 us
    pallas_call x2, Pallas kernels, attend_back(): call(attend_back_kernel, shape((blocks, qkv_cols, block)), grid=(seqs,),...  18.9 us
  transfers between devices with their start and end apart: 68, of which 29 were waited for; matrix products, arithmetic and copies ran while one was open for 11% of the time, Pallas kernels for 19%

profile of v1, /device:TPU:0, one launch (start us, length us, event | category | flops | bytes accessed | tf_op | source)
XLA Modules:
  0.0 530.8 jit_solution(14504141285938738746)
XLA Ops:
  10.8 3.0 shard_map.229
  13.8 3.1 collective-permute-start
  17.0 4.1 copy.33
  21.1 2.6 bitcast_reduce_fusion
  30.2 4.1 collective-permute-done.1.refs_2_
  37.1 4.9 collective-permute-done.5.refs_6_
  48.5 2.8 shard_map.230
  52.2 6.6 %collective-permute-done.8.refs_1_ = bf16[128,2304]{1,0:T(8,128)(2,1)S(1)} collective-permute-done((bf16[128,2304]{1,0:T(8,128)(2,1)S(1)}, bf16[128,2304]{1,0:T(8,128)(2,1)S(1)}, u32[]{:S(2)}, u32[]{:S(2)}) %collective-permute-start.8) | collective-permute-done | bytes 589856 | tf_op jit(solution)/shard_map/ppermute | solution.py:119
  61.4 9.4 %shard_map.231 = (bf16[768,1024]{1,0:T(8,128)(2,1)}, bf16[4,256,256]{2,1,0:T(8,128)(2,1)}, f32[8,1024]{1,0:T(8,128)}) custom-call(bf16[4,1024,256]{2,1,0:T(8,128)(2,1)} %multiply_convert_fusion.x.refs_0_, bf16[1024,768]{1,0:T(8,128)(2,1)} %bitcast.117, f32[1,768]{1,0:T(1,128)} %get-tuple-element.145.bias, f32[8,512]{1,0:T(8,128)} %get-tuple-element.149.cosine, ...), custom_call_target="tpu_custom_call" | custom-call | flops 2147483648 | bytes 3670016 | tf_op jit(solution)/shard_map/pallas_call | solution.py:590
  71.8 2.1 collective-permute-done.11.refs_7_
  75.9 11.4 %collective-permute-done.13.refs_6_ = bf16[128,2304]{1,0:T(8,128)(2,1)S(1)} collective-permute-done((bf16[128,2304]{1,0:T(8,128)(2,1)S(1)}, bf16[128,2304]{1,0:T(8,128)(2,1)S(1)}, u32[]{:S(2)}, u32[]{:S(2)}) %collective-permute-start.13) | collective-permute-done | bytes 589856 | tf_op jit(solution)/shard_map/ppermute | solution.py:118
  90.8 3.2 collective-permute-done.14.refs_4_
  95.5 4.8 shard_map.232
  100.4 8.6 %shard_map.233 = (bf16[4,1024,256]{2,1,0:T(8,128)(2,1)}, bf16[4,1024,256]{2,1,0:T(8,128)(2,1)}) custom-call(bf16[4,1024,256]{2,1,0:T(8,128)(2,1)} %multiply_convert_fusion.x.refs_0_, bf16[1024,2304]{1,0:T(8,128)(2,1)} %bitcast.88, f32[1,1024]{1,0:T(1,128)} %get-tuple-element.143.bias), custom_call_target="tpu_custom_call" | custom-call | flops 2147483648 | bytes 8388608 | tf_op jit(solution)/shard_map/pallas_call | solution.py:613
  108.9 7.3 %shard_map.234 = bf16[4,1024,256]{2,1,0:T(8,128)(2,1)} custom-call(bf16[4,256,256]{2,1,0:T(8,128)(2,1)} %get-tuple-element.71.mixed.refs_3_, bf16[4,1024,256]{2,1,0:T(8,128)(2,1)} %get-tuple-element.76.hidden.refs_4_, bf16[1024,2304]{1,0:T(8,128)(2,1)} %bitcast.89), custom_call_target="tpu_custom_call" | custom-call | flops 2684354560 | bytes 7340032 | tf_op jit(solution)/shard_map/pallas_call | solution.py:626
  117.6 2.6 collective-permute-done.16
  127.2 8.5 %collective-permute-done.17 = bf16[1,1024,256]{2,1,0:T(8,128)(2,1)S(1)} collective-permute-done((bf16[1,1024,256]{2,1,0:T(8,128)(2,1)S(1)}, bf16[1,1024,256]{2,1,0:T(8,128)(2,1)S(1)}, u32[]{:S(2)}, u32[]{:S(2)}) %collective-permute-start.17) | collective-permute-done | bytes 524320 | tf_op jit(solution)/shard_map/ppermute | solution.py:192
  138.5 2.7 fusion.12
  144.8 9.7 %collective-permute-done.21.refs_2_ = bf16[128,1792]{1,0:T(8,128)(2,1)S(1)} collective-permute-done((bf16[128,1792]{1,0:T(8,128)(2,1)}, bf16[128,1792]{1,0:T(8,128)(2,1)S(1)}, u32[]{:S(2)}, u32[]{:S(2)}) %collective-permute-start.21) | collective-permute-done | bytes 458784 | tf_op jit(solution)/shard_map/ppermute | solution.py:119
  159.3 5.9 %collective-permute-done.31.refs_8_ = bf16[128,1280]{1,0:T(8,128)(2,1)S(1)} collective-permute-done((bf16[128,1280]{1,0:T(8,128)(2,1)S(1)}, bf16[128,1280]{1,0:T(8,128)(2,1)S(1)}, u32[]{:S(2)}, u32[]{:S(2)}) %collective-permute-start.31) | collective-permute-done | bytes 327712 | tf_op jit(solution)/shard_map/ppermute | solution.py:118
  169.3 6.5 %collective-permute-done.32.refs_7_ = bf16[128,1280]{1,0:T(8,128)(2,1)S(1)} collective-permute-done((bf16[128,1280]{1,0:T(8,128)(2,1)S(1)}, bf16[128,1280]{1,0:T(8,128)(2,1)S(1)}, u32[]{:S(2)}, u32[]{:S(2)}) %collective-permute-start.32) | collective-permute-done | bytes 327712 | tf_op jit(solution)/shard_map/ppermute | solution.py:118
  177.9 7.8 %collective-permute-done.25.refs_6_ = bf16[128,1792]{1,0:T(8,128)(2,1)S(1)} collective-permute-done((bf16[128,1792]{1,0:T(8,128)(2,1)S(1)}, bf16[128,1792]{1,0:T(8,128)(2,1)S(1)}, u32[]{:S(2)}, u32[]{:S(2)}) %collective-permute-start.25) | collective-permute-done | bytes 458784 | tf_op jit(solution)/shard_map/ppermute | solution.py:118
  190.7 2.0 collective-permute-done.33.refs_6_
  196.9 4.0 copy.38
  200.9 4.0 shard_map.235
  205.0 3.3 shard_map.238
  209.9 9.3 %shard_map.236 = (bf16[768,1024]{1,0:T(8,128)(2,1)}, bf16[4,256,256]{2,1,0:T(8,128)(2,1)}, f32[8,1024]{1,0:T(8,128)}) custom-call(bf16[4,1024,256]{2,1,0:T(8,128)(2,1)} %maximum_select_fusion.x.refs_0_, bf16[1024,1792]{1,0:T(8,128)(2,1)} %bitcast.92, f32[1,768]{1,0:T(1,128)} %get-tuple-element.144.bias, f32[8,512]{1,0:T(8,128)} %get-tuple-element.149.cosine, ...), custom_call_target="tpu_custom_call" | custom-call | flops 2147483648 | bytes 3670016 | tf_op jit(solution)/shard_map/pallas_call | solution.py:590
  219.3 8.3 %shard_map.237 = (bf16[4,1024,256]{2,1,0:T(8,128)(2,1)}, bf16[4,1024,256]{2,1,0:T(8,128)(2,1)}) custom-call(bf16[4,1024,256]{2,1,0:T(8,128)(2,1)} %maximum_select_fusion.x.refs_0_, bf16[1024,1792]{1,0:T(8,128)(2,1)} %bitcast.93, f32[1,1024]{1,0:T(1,128)} %get-tuple-element.141.bias), custom_call_target="tpu_custom_call" | custom-call | flops 2147483648 | bytes 8388608 | tf_op jit(solution)/shard_map/pallas_call | solution.py:613
  227.6 7.7 %shard_map.239 = (bf16[4,256,256]{2,1,0:T(8,128)(2,1)}, bf16[4,1024,256]{2,1,0:T(8,128)(2,1)}) custom-call(bf16[4,1024,256]{2,1,0:T(8,128)(2,1)} %bitcast.96, bf16[1024,1280]{1,0:T(8,128)(2,1)} %bitcast.99, bf16[4,1024,256]{2,1,0:T(8,128)(2,1)} %get-tuple-element.87.slope), custom_call_target="tpu_custom_call" | custom-call | flops 2684354560 | bytes 9961472 | tf_op jit(solution)/shard_map/pallas_call | solution.py:638
  235.3 9.3 %shard_map.240.d_joined.refs_2_ = bf16[4,768,256]{2,1,0:T(8,128)(2,1)} custom-call(bf16[768,1024]{1,0:T(8,128)(2,1)} %get-tuple-element.83.qkv, f32[8,1024]{1,0:T(8,128)} %get-tuple-element.84.log_total, bf16[4,256,256]{2,1,0:T(8,128)(2,1)} %get-tuple-element.88.d_mixed, f32[8,512]{1,0:T(8,128)} %get-tuple-element.149.cosine, f32[8,512]{1,0:T(8,128)} %get-tuple-element.148.sine), custom_call_target="tpu_custom_call" | custom-call | flops 1342177280 | bytes 4718592 | tf_op jit(solution)/shard_map/pallas_call | solution.py:650
  244.6 8.4 %shard_map.241 = bf16[4,1024,256]{2,1,0:T(8,128)(2,1)} custom-call(bf16[4,768,256]{2,1,0:T(8,128)(2,1)} %shard_map.240.d_joined.refs_2_, bf16[4,1024,256]{2,1,0:T(8,128)(2,1)} %get-tuple-element.89.d_hidden.refs_3_, bf16[1024,1792]{1,0:T(8,128)(2,1)} %bitcast.94, bf16[1024,1792]{1,0:T(8,128)(2,1)} %bitcast.95), custom_call_target="tpu_custom_call" | custom-call | flops 3758096384 | bytes 9437184 | tf_op jit(solution)/shard_map/pallas_call | solution.py:669
  254.5 2.6 collective-permute-done.36
  258.3 15.9 %shard_map.242 = bf16[8,144,3072]{2,1,0:T(8,128)(2,1)} custom-call(bf16[4,1024,256]{2,1,0:T(8,128)(2,1)} %maximum_select_fusion.x.refs_0_, bf16[4,1024,256]{2,1,0:T(8,128)(2,1)} %bitcast.97, bf16[4,768,256]{2,1,0:T(8,128)(2,1)} %shard_map.240.d_joined.refs_2_, bf16[4,1024,256]{2,1,0:T(8,128)(2,1)} %get-tuple-element.89.d_hidden.refs_3_, ...), custom_call_target="tpu_custom_call" | custom-call | flops 6442450944 | bytes 14680064 | tf_op jit(solution)/shard_map/pallas_call | solution.py:689
  274.2 6.9 %shard_map.243 = bf16[4,1024,256]{2,1,0:T(8,128)(2,1)} custom-call(bf16[4,256,256]{2,1,0:T(8,128)(2,1)} %get-tuple-element.81.refs_4_.mixed, bf16[4,1024,256]{2,1,0:T(8,128)(2,1)} %get-tuple-element.91.refs_5_.hidden, bf16[1024,1280]{1,0:T(8,128)(2,1)} %bitcast.100), custom_call_target="tpu_custom_call" | custom-call | flops 2684354560 | bytes 7340032 | tf_op jit(solution)/shard_map/pallas_call | solution.py:626
  283.1 13.8 %collective-permute-done.41 = bf16[1,1024,256]{2,1,0:T(8,128)(2,1)S(1)} collective-permute-done((bf16[1,1024,256]{2,1,0:T(8,128)(2,1)S(1)}, bf16[1,1024,256]{2,1,0:T(8,128)(2,1)S(1)}, u32[]{:S(2)}, u32[]{:S(2)}) %collective-permute-start.41) | collective-permute-done | bytes 524320 | tf_op jit(solution)/shard_map/ppermute | solution.py:192
  298.2 12.9 %collective-permute-done.38 = bf16[1,1024,256]{2,1,0:T(8,128)(2,1)S(1)} collective-permute-done((bf16[1,1024,256]{2,1,0:T(8,128)(2,1)S(1)}, bf16[1,1024,256]{2,1,0:T(8,128)(2,1)S(1)}, u32[]{:S(2)}, u32[]{:S(2)}) %collective-permute-start.38) | collective-permute-done | bytes 524320 | tf_op jit(solution)/shard_map/ppermute | solution.py:192
  311.1 2.4 fusion.18
  313.9 12.5 %collective-permute-done.42 = bf16[1,1024,256]{2,1,0:T(8,128)(2,1)S(1)} collective-permute-done((bf16[1,1024,256]{2,1,0:T(8,128)(2,1)S(1)}, bf16[1,1024,256]{2,1,0:T(8,128)(2,1)S(1)}, u32[]{:S(2)}, u32[]{:S(2)}) %collective-permute-start.42) | collective-permute-done | bytes 524320 | tf_op jit(solution)/shard_map/ppermute | solution.py:210
  326.6 2.6 collective-permute-done.43
  330.9 8.3 %shard_map.244 = (bf16[4,256,256]{2,1,0:T(8,128)(2,1)}, bf16[4,1024,256]{2,1,0:T(8,128)(2,1)}) custom-call(bf16[4,1024,256]{2,1,0:T(8,128)(2,1)} %maximum_select_fusion.2.grad.refs_1_.refs_3_, bf16[1024,2304]{1,0:T(8,128)(2,1)} %bitcast.90, bf16[4,1024,256]{2,1,0:T(8,128)(2,1)} %get-tuple-element.94.slope), custom_call_target="tpu_custom_call" | custom-call | flops 2684354560 | bytes 9961472 | tf_op jit(solution)/shard_map/pallas_call | solution.py:638
  339.2 9.9 %shard_map.245.up_piece.down_piece.piece = bf16[8,128,2304]{2,1,0:T(8,128)(2,1)} custom-call(bf16[4,1024,256]{2,1,0:T(8,128)(2,1)} %multiply_convert_fusion.x.refs_0_, bf16[4,1024,256]{2,1,0:T(8,128)(2,1)} %maximum_select_fusion.2.grad.refs_1_.refs_3_, bf16[4,1024,256]{2,1,0:T(8,128)(2,1)} %get-tuple-element.96.refs_2_.d_hidden, ...), custom_call_target="tpu_custom_call" | custom-call | flops 4831838208 | bytes 11534336 | tf_op jit(solution)/shard_map/pallas_call | solution.py:689
  349.0 9.6 %shard_map.246.refs_1_.d_joined = bf16[4,768,256]{2,1,0:T(8,128)(2,1)} custom-call(bf16[768,1024]{1,0:T(8,128)(2,1)} %get-tuple-element.92.qkv, f32[8,1024]{1,0:T(8,128)} %get-tuple-element.93.log_total, bf16[4,256,256]{2,1,0:T(8,128)(2,1)} %get-tuple-element.97.d_mixed, f32[8,512]{1,0:T(8,128)} %get-tuple-element.149.cosine, f32[8,512]{1,0:T(8,128)} %get-tuple-element.148.sine), custom_call_target="tpu_custom_call" | custom-call | flops 1342177280 | bytes 4718592 | tf_op jit(solution)/shard_map/pallas_call | solution.py:650
  358.6 9.0 %shard_map.247.up_piece.down_piece.piece = bf16[8,144,768]{2,1,0:T(8,128)(2,1)} custom-call(bf16[4,1024,256]{2,1,0:T(8,128)(2,1)} %multiply_convert_fusion.x.refs_0_, bf16[4,768,256]{2,1,0:T(8,128)(2,1)} %shard_map.246.refs_1_.d_joined, bf16[4,1024,256]{2,1,0:T(8,128)(2,1)} %get-tuple-element.96.refs_2_.d_hidden, ...), custom_call_target="tpu_custom_call" | custom-call | flops 1610612736 | bytes 5242880 | tf_op jit(solution)/shard_map/pallas_call | solution.py:689
  367.6 9.3 %shard_map.248 = bf16[4,1024,256]{2,1,0:T(8,128)(2,1)} custom-call(bf16[4,768,256]{2,1,0:T(8,128)(2,1)} %shard_map.246.refs_1_.d_joined, bf16[4,1024,256]{2,1,0:T(8,128)(2,1)} %get-tuple-element.96.refs_2_.d_hidden, bf16[1024,768]{1,0:T(8,128)(2,1)} %bitcast.118, bf16[1024,2304]{1,0:T(8,128)(2,1)} %bitcast.91), custom_call_target="tpu_custom_call" | custom-call | flops 3758096384 | bytes 9437184 | tf_op jit(solution)/shard_map/pallas_call | solution.py:669
  388.8 9.9 %collective-permute-done.56.left = bf16[128,1152]{1,0:T(8,128)(2,1)S(1)} collective-permute-done((bf16[128,1152]{1,0:T(8,128)(2,1)S(1)}, bf16[128,1152]{1,0:T(8,128)(2,1)S(1)}, u32[]{:S(2)}, u32[]{:S(2)}) %collective-permute-start.56) | collective-permute-done | bytes 294944 | tf_op jit(solution)/shard_map/ppermute | solution.py:161
  398.7 6.7 %collective-permute-done.57.right = bf16[128,1152]{1,0:T(8,128)(2,1)} collective-permute-done((bf16[128,1152]{1,0:T(8,128)(2,1)S(1)}, bf16[128,1152]{1,0:T(8,128)(2,1)}, u32[]{:S(2)}, u32[]{:S(2)}) %collective-permute-start.57) | collective-permute-done | bytes 294944 | tf_op jit(solution)/shard_map/ppermute | solution.py:162
  405.4 3.7 shard_map.254
  419.1 8.2 %collective-permute-done.48.left = bf16[144,384]{1,0:T(8,128)(2,1)S(1)} collective-permute-done((bf16[144,384]{1,0:T(8,128)(2,1)S(1)}, bf16[144,384]{1,0:T(8,128)(2,1)S(1)}, u32[]{:S(2)}, u32[]{:S(2)}) %collective-permute-start.48) | collective-permute-done | bytes 110624 | tf_op jit(solution)/shard_map/ppermute | solution.py:161
  428.6 2.6 shard_map.249
  432.4 3.4 shard_map.255
  437.8 2.3 maximum_select_fusion.7
  441.5 14.7 %collective-permute-done.51.down_in = bf16[144,768]{1,0:T(8,128)(2,1)S(1)} collective-permute-done((bf16[144,768]{1,0:T(8,128)(2,1)S(1)}, bf16[144,768]{1,0:T(8,128)(2,1)S(1)}, u32[]{:S(2)}, u32[]{:S(2)}) %collective-permute-start.51) | collective-permute-done | bytes 221216 | tf_op jit(solution)/shard_map/ppermute | solution.py:167
  456.9 2.7 shard_map.250
  463.0 3.4 shard_map.256
  468.7 16.6 %collective-permute-done.53.down_in = bf16[144,768]{1,0:T(8,128)(2,1)S(1)} collective-permute-done((bf16[144,768]{1,0:T(8,128)(2,1)S(1)}, bf16[144,768]{1,0:T(8,128)(2,1)S(1)}, u32[]{:S(2)}, u32[]{:S(2)}) %collective-permute-start.53) | collective-permute-done | bytes 221216 | tf_op jit(solution)/shard_map/ppermute | solution.py:167
  486.0 2.7 shard_map.251
  491.7 2.1 fusion
  493.8 2.6 copy.39
  496.5 3.3 shard_map.257.refs_1_
  499.8 2.6 fusion.1
  502.4 2.4 copy.41
  504.7 4.4 shard_map.252
  509.8 2.6 shard_map.253.refs_0_
  512.5 4.7 shard_map.258
  (304 shorter events, 118.4 us)
Async XLA Ops:
  7.2 497.6 %reduce-scatter.2.cloned.1.call-start = ((), (), s32[]{:S(2)}) async-start(), calls=%async_computation.1 | async-start | bytes 7962624 | tf_op jit(solution)/shard_map/reduce_scatter | solution.py:747
  13.8 13.5 %collective-permute-start = (bf16[144,768]{1,0:T(8,128)(2,1)}, bf16[144,768]{1,0:T(8,128)(2,1)S(1)}, u32[]{:S(2)}, u32[]{:S(2)}) collective-permute-start(bf16[144,768]{1,0:T(8,128)(2,1)} %get-tuple-element.68.refs_0_), channel_id=1, source_target_pairs={{8,0},{16,8},{24,16},{28,24},{20,28},{12,20},{4,12},{0,4},{9,1},{1... | collective-permute-start | bytes 663560 | tf_op jit(solution)/shard_map/ppermute | solution.py:119
  16.9 12.5 %collective-permute-start.3 = (bf16[144,768]{1,0:T(8,128)(2,1)}, bf16[144,768]{1,0:T(8,128)(2,1)S(1)}, u32[]{:S(2)}, u32[]{:S(2)}) collective-permute-start(bf16[144,768]{1,0:T(8,128)(2,1)} %get-tuple-element.68.refs_0_), channel_id=1, source_target_pairs={{0,8},{8,16},{16,24},{24,28},{28,20},{20,12},{12,4},{4,0},{1,9},{9... | collective-permute-start | bytes 663560 | tf_op jit(solution)/shard_map/ppermute | solution.py:118
  27.3 6.9 %collective-permute-start.1 = (bf16[144,768]{1,0:T(8,128)(2,1)S(1)}, bf16[144,768]{1,0:T(8,128)(2,1)S(1)}, u32[]{:S(2)}, u32[]{:S(2)}) collective-permute-start(bf16[144,768]{1,0:T(8,128)(2,1)S(1)} %collective-permute-done.refs_1_), channel_id=1, source_target_pairs={{8,0},{16,8},{24,16},{28,24},{20,28},{12,20},{4,12},{0,4},{9,1},{1... | collective-permute-start | bytes 663560 | tf_op jit(solution)/shard_map/ppermute | solution.py:119
  29.3 6.6 %collective-permute-start.4 = (bf16[144,768]{1,0:T(8,128)(2,1)S(1)}, bf16[144,768]{1,0:T(8,128)(2,1)S(1)}, u32[]{:S(2)}, u32[]{:S(2)}) collective-permute-start(bf16[144,768]{1,0:T(8,128)(2,1)S(1)} %collective-permute-done.3.refs_8_), channel_id=1, source_target_pairs={{0,8},{8,16},{16,24},{24,28},{28,20},{20,12},{12,4},{4,0},{1,9},{9... | collective-permute-start | bytes 663560 | tf_op jit(solution)/shard_map/ppermute | solution.py:118
  34.3 8.0 %collective-permute-start.2 = (bf16[144,768]{1,0:T(8,128)(2,1)S(1)}, bf16[144,768]{1,0:T(8,128)(2,1)S(1)}, u32[]{:S(2)}, u32[]{:S(2)}) collective-permute-start(bf16[144,768]{1,0:T(8,128)(2,1)S(1)} %collective-permute-done.1.refs_2_), channel_id=1, source_target_pairs={{8,0},{16,8},{24,16},{28,24},{20,28},{12,20},{4,12},{0,4},{9,1},{1... | collective-permute-start | bytes 663560 | tf_op jit(solution)/shard_map/ppermute | solution.py:119
  36.0 6.0 %collective-permute-start.5 = (bf16[144,768]{1,0:T(8,128)(2,1)S(1)}, bf16[144,768]{1,0:T(8,128)(2,1)S(1)}, u32[]{:S(2)}, u32[]{:S(2)}) collective-permute-start(bf16[144,768]{1,0:T(8,128)(2,1)S(1)} %collective-permute-done.4.refs_7_), channel_id=1, source_target_pairs={{0,8},{8,16},{16,24},{24,28},{28,20},{20,12},{12,4},{4,0},{1,9},{9... | collective-permute-start | bytes 663560 | tf_op jit(solution)/shard_map/ppermute | solution.py:118
  42.0 5.7 %collective-permute-start.6 = (bf16[144,384]{1,0:T(8,128)(2,1)S(1)}, bf16[144,384]{1,0:T(8,128)(2,1)S(1)}, u32[]{:S(2)}, u32[]{:S(2)}) collective-permute-start(bf16[144,384]{1,0:T(8,128)(2,1)S(1)} %slice.105), channel_id=1, source_target_pairs={{0,8},{8,16},{16,24},{24,28},{28,20},{20,12},{12,4},{4,0},{1,9},{9... | collective-permute-start | bytes 331784 | tf_op jit(solution)/shard_map/ppermute | solution.py:123
  42.4 6.1 %collective-permute-start.7 = (bf16[144,384]{1,0:T(8,128)(2,1)S(1)}, bf16[144,384]{1,0:T(8,128)(2,1)}, u32[]{:S(2)}, u32[]{:S(2)}) collective-permute-start(bf16[144,384]{1,0:T(8,128)(2,1)S(1)} %slice.106), channel_id=1, source_target_pairs={{8,0},{16,8},{24,16},{28,24},{20,28},{12,20},{4,12},{0,4},{9,1},{1... | collective-permute-start | bytes 331784 | tf_op jit(solution)/shard_map/ppermute | solution.py:124
  45.3 13.5 %collective-permute-start.8 = (bf16[128,2304]{1,0:T(8,128)(2,1)S(1)}, bf16[128,2304]{1,0:T(8,128)(2,1)S(1)}, u32[]{:S(2)}, u32[]{:S(2)}) collective-permute-start(bf16[128,2304]{1,0:T(8,128)(2,1)S(1)} %copy-done.15), channel_id=1, source_target_pairs={{8,0},{16,8},{24,16},{28,24},{20,28},{12,20},{4,12},{0,4},{9,1},{1... | collective-permute-start | bytes 1769480 | tf_op jit(solution)/shard_map/ppermute | solution.py:119
  46.9 13.5 %collective-permute-start.10 = (bf16[128,2304]{1,0:T(8,128)(2,1)S(1)}, bf16[128,2304]{1,0:T(8,128)(2,1)S(1)}, u32[]{:S(2)}, u32[]{:S(2)}) collective-permute-start(bf16[128,2304]{1,0:T(8,128)(2,1)S(1)} %copy-done.15), channel_id=1, source_target_pairs={{0,8},{8,16},{16,24},{24,28},{28,20},{20,12},{12,4},{4,0},{1,9},{9... | collective-permute-start | bytes 1769480 | tf_op jit(solution)/shard_map/ppermute | solution.py:118
  58.8 13.0 %collective-permute-start.9 = (bf16[128,2304]{1,0:T(8,128)(2,1)S(1)}, bf16[128,2304]{1,0:T(8,128)(2,1)S(1)}, u32[]{:S(2)}, u32[]{:S(2)}) collective-permute-start(bf16[128,2304]{1,0:T(8,128)(2,1)S(1)} %collective-permute-done.8.refs_1_), channel_id=1, source_target_pairs={{8,0},{16,8},{24,16},{28,24},{20,28},{12,20},{4,12},{0,4},{9,1},{1... | collective-permute-start | bytes 1769480 | tf_op jit(solution)/shard_map/ppermute | solution.py:119
  60.4 13.5 %collective-permute-start.11 = (bf16[128,2304]{1,0:T(8,128)(2,1)S(1)}, bf16[128,2304]{1,0:T(8,128)(2,1)S(1)}, u32[]{:S(2)}, u32[]{:S(2)}) collective-permute-start(bf16[128,2304]{1,0:T(8,128)(2,1)S(1)} %collective-permute-done.10.refs_8_), channel_id=1, source_target_pairs={{0,8},{8,16},{16,24},{24,28},{28,20},{20,12},{12,4},{4,0},{1,9},{9... | collective-permute-start | bytes 1769480 | tf_op jit(solution)/shard_map/ppermute | solution.py:118
  73.8 13.4 %collective-permute-start.13 = (bf16[128,2304]{1,0:T(8,128)(2,1)S(1)}, bf16[128,2304]{1,0:T(8,128)(2,1)S(1)}, u32[]{:S(2)}, u32[]{:S(2)}) collective-permute-start(bf16[128,2304]{1,0:T(8,128)(2,1)S(1)} %collective-permute-done.11.refs_7_), channel_id=1, source_target_pairs={{0,8},{8,16},{16,24},{24,28},{28,20},{20,12},{12,4},{4,0},{1,9},{9... | collective-permute-start | bytes 1769480 | tf_op jit(solution)/shard_map/ppermute | solution.py:118
  74.2 13.5 %collective-permute-start.12 = (bf16[128,2304]{1,0:T(8,128)(2,1)S(1)}, bf16[128,2304]{1,0:T(8,128)(2,1)S(1)}, u32[]{:S(2)}, u32[]{:S(2)}) collective-permute-start(bf16[128,2304]{1,0:T(8,128)(2,1)S(1)} %collective-permute-done.9.refs_2_), channel_id=1, source_target_pairs={{8,0},{16,8},{24,16},{28,24},{20,28},{12,20},{4,12},{0,4},{9,1},{1... | collective-permute-start | bytes 1769480 | tf_op jit(solution)/shard_map/ppermute | solution.py:119
  87.3 6.8 %collective-permute-start.14 = (bf16[128,1152]{1,0:T(8,128)(2,1)S(1)}, bf16[128,1152]{1,0:T(8,128)(2,1)S(1)}, u32[]{:S(2)}, u32[]{:S(2)}) collective-permute-start(bf16[128,1152]{1,0:T(8,128)(2,1)S(1)} %slice.110), channel_id=1, source_target_pairs={{0,8},{8,16},{16,24},{24,28},{28,20},{20,12},{12,4},{4,0},{1,9},{9... | collective-permute-start | bytes 884744 | tf_op jit(solution)/shard_map/ppermute | solution.py:123
  87.7 6.8 %collective-permute-start.15 = (bf16[128,1152]{1,0:T(8,128)(2,1)S(1)}, bf16[128,1152]{1,0:T(8,128)(2,1)S(1)}, u32[]{:S(2)}, u32[]{:S(2)}) collective-permute-start(bf16[128,1152]{1,0:T(8,128)(2,1)S(1)} %slice.111), channel_id=1, source_target_pairs={{8,0},{16,8},{24,16},{28,24},{20,28},{12,20},{4,12},{0,4},{9,1},{1... | collective-permute-start | bytes 884744 | tf_op jit(solution)/shard_map/ppermute | solution.py:124
  121.8 14.0 %collective-permute-start.17 = (bf16[1,1024,256]{2,1,0:T(8,128)(2,1)S(1)}, bf16[1,1024,256]{2,1,0:T(8,128)(2,1)S(1)}, u32[]{:S(2)}, u32[]{:S(2)}) collective-permute-start(bf16[1,1024,256]{2,1,0:T(8,128)(2,1)S(1)} %dynamic-slice_convert_fusion.2), channel_id=1, source_target_pairs={{0,2},{1,3},{2,0},{3,1},{4,6},{5,7},{6,4},{7,5},{8,10},{9,11},{10,... | collective-permute-start | bytes 1572872 | tf_op jit(solution)/shard_map/ppermute | solution.py:192
  124.7 18.0 %collective-permute-start.20 = (bf16[128,1792]{1,0:T(8,128)(2,1)}, bf16[128,1792]{1,0:T(8,128)(2,1)}, u32[]{:S(2)}, u32[]{:S(2)}) collective-permute-start(bf16[128,1792]{1,0:T(8,128)(2,1)} %get-tuple-element.78.refs_0_), channel_id=1, source_target_pairs={{8,0},{16,8},{24,16},{28,24},{20,28},{12,20},{4,12},{0,4},{9,1},{1... | collective-permute-start | bytes 1376264 | tf_op jit(solution)/shard_map/ppermute | solution.py:119
  126.4 18.0 %collective-permute-start.22 = (bf16[128,1792]{1,0:T(8,128)(2,1)}, bf16[128,1792]{1,0:T(8,128)(2,1)}, u32[]{:S(2)}, u32[]{:S(2)}) collective-permute-start(bf16[128,1792]{1,0:T(8,128)(2,1)} %get-tuple-element.78.refs_0_), channel_id=1, source_target_pairs={{0,8},{8,16},{16,24},{24,28},{28,20},{20,12},{12,4},{4,0},{1,9},{9... | collective-permute-start | bytes 1376264 | tf_op jit(solution)/shard_map/ppermute | solution.py:118
  141.2 16.6 %collective-permute-start.18 = (bf16[1,1024,256]{2,1,0:T(8,128)(2,1)}, bf16[1,1024,256]{2,1,0:T(8,128)(2,1)S(1)}, u32[]{:S(2)}, u32[]{:S(2)}) collective-permute-start(bf16[1,1024,256]{2,1,0:T(8,128)(2,1)} %get-tuple-element.126), channel_id=1, source_target_pairs={{0,2},{1,3},{2,0},{3,1},{4,6},{5,7},{6,4},{7,5},{8,10},{9,11},{10,... | collective-permute-start | bytes 1572872 | tf_op jit(solution)/shard_map/ppermute | solution.py:210
  142.8 11.7 %collective-permute-start.21 = (bf16[128,1792]{1,0:T(8,128)(2,1)}, bf16[128,1792]{1,0:T(8,128)(2,1)S(1)}, u32[]{:S(2)}, u32[]{:S(2)}) collective-permute-start(bf16[128,1792]{1,0:T(8,128)(2,1)} %collective-permute-done.20.refs_1_), channel_id=1, source_target_pairs={{8,0},{16,8},{24,16},{28,24},{20,28},{12,20},{4,12},{0,4},{9,1},{1... | collective-permute-start | bytes 1376264 | tf_op jit(solution)/shard_map/ppermute | solution.py:119
  144.3 11.5 %collective-permute-start.23 = (bf16[128,1792]{1,0:T(8,128)(2,1)}, bf16[128,1792]{1,0:T(8,128)(2,1)S(1)}, u32[]{:S(2)}, u32[]{:S(2)}) collective-permute-start(bf16[128,1792]{1,0:T(8,128)(2,1)} %collective-permute-done.22.refs_8_), channel_id=1, source_target_pairs={{0,8},{8,16},{16,24},{24,28},{28,20},{20,12},{12,4},{4,0},{1,9},{9... | collective-permute-start | bytes 1376264 | tf_op jit(solution)/shard_map/ppermute | solution.py:118
  155.8 9.9 %collective-permute-start.28 = (bf16[128,1280]{1,0:T(8,128)(2,1)S(1)}, bf16[128,1280]{1,0:T(8,128)(2,1)S(1)}, u32[]{:S(2)}, u32[]{:S(2)}) collective-permute-start(bf16[128,1280]{1,0:T(8,128)(2,1)S(1)} %copy-done.28), channel_id=1, source_target_pairs={{8,0},{16,8},{24,16},{28,24},{20,28},{12,20},{4,12},{0,4},{9,1},{1... | collective-permute-start | bytes 983048 | tf_op jit(solution)/shard_map/ppermute | solution.py:119
  157.4 7.9 %collective-permute-start.31 = (bf16[128,1280]{1,0:T(8,128)(2,1)S(1)}, bf16[128,1280]{1,0:T(8,128)(2,1)S(1)}, u32[]{:S(2)}, u32[]{:S(2)}) collective-permute-start(bf16[128,1280]{1,0:T(8,128)(2,1)S(1)} %copy-done.28), channel_id=1, source_target_pairs={{0,8},{8,16},{16,24},{24,28},{28,20},{20,12},{12,4},{4,0},{1,9},{9... | collective-permute-start | bytes 983048 | tf_op jit(solution)/shard_map/ppermute | solution.py:118
  159.3 49.0 %collective-permute-start.19 = (bf16[2,1024,256]{2,1,0:T(8,128)(2,1)S(1)}, bf16[2,1024,256]{2,1,0:T(8,128)(2,1)S(1)}, u32[]{:S(2)}, u32[]{:S(2)}) collective-permute-start(bf16[2,1024,256]{2,1,0:T(8,128)(2,1)S(1)} %maximum_select_fusion.4), channel_id=1, source_target_pairs={{0,1},{1,0},{2,3},{3,2},{4,5},{5,4},{6,7},{7,6},{8,9},{9,8},{10,11... | collective-permute-start | bytes 3145736 | tf_op jit(solution)/shard_map/ppermute | solution.py:210
  165.2 10.6 %collective-permute-start.32 = (bf16[128,1280]{1,0:T(8,128)(2,1)S(1)}, bf16[128,1280]{1,0:T(8,128)(2,1)S(1)}, u32[]{:S(2)}, u32[]{:S(2)}) collective-permute-start(bf16[128,1280]{1,0:T(8,128)(2,1)S(1)} %collective-permute-done.31.refs_8_), channel_id=1, source_target_pairs={{0,8},{8,16},{16,24},{24,28},{28,20},{20,12},{12,4},{4,0},{1,9},{9... | collective-permute-start | bytes 983048 | tf_op jit(solution)/shard_map/ppermute | solution.py:118
  165.7 10.6 %collective-permute-start.29 = (bf16[128,1280]{1,0:T(8,128)(2,1)S(1)}, bf16[128,1280]{1,0:T(8,128)(2,1)S(1)}, u32[]{:S(2)}, u32[]{:S(2)}) collective-permute-start(bf16[128,1280]{1,0:T(8,128)(2,1)S(1)} %collective-permute-done.28.refs_1_), channel_id=1, source_target_pairs={{8,0},{16,8},{24,16},{28,24},{20,28},{12,20},{4,12},{0,4},{9,1},{1... | collective-permute-start | bytes 983048 | tf_op jit(solution)/shard_map/ppermute | solution.py:119
  167.3 18.4 %collective-permute-start.25 = (bf16[128,1792]{1,0:T(8,128)(2,1)S(1)}, bf16[128,1792]{1,0:T(8,128)(2,1)S(1)}, u32[]{:S(2)}, u32[]{:S(2)}) collective-permute-start(bf16[128,1792]{1,0:T(8,128)(2,1)S(1)} %copy-done.27), channel_id=1, source_target_pairs={{0,8},{8,16},{16,24},{24,28},{28,20},{20,12},{12,4},{4,0},{1,9},{9... | collective-permute-start | bytes 1376264 | tf_op jit(solution)/shard_map/ppermute | solution.py:118
  167.7 19.9 %collective-permute-start.24 = (bf16[128,1792]{1,0:T(8,128)(2,1)}, bf16[128,1792]{1,0:T(8,128)(2,1)S(1)}, u32[]{:S(2)}, u32[]{:S(2)}) collective-permute-start(bf16[128,1792]{1,0:T(8,128)(2,1)} %copy-done.25), channel_id=1, source_target_pairs={{8,0},{16,8},{24,16},{28,24},{20,28},{12,20},{4,12},{0,4},{9,1},{1... | collective-permute-start | bytes 1376264 | tf_op jit(solution)/shard_map/ppermute | solution.py:119
  175.8 16.9 %collective-permute-start.33 = (bf16[128,1280]{1,0:T(8,128)(2,1)S(1)}, bf16[128,1280]{1,0:T(8,128)(2,1)S(1)}, u32[]{:S(2)}, u32[]{:S(2)}) collective-permute-start(bf16[128,1280]{1,0:T(8,128)(2,1)S(1)} %collective-permute-done.32.refs_7_), channel_id=1, source_target_pairs={{0,8},{8,16},{16,24},{24,28},{28,20},{20,12},{12,4},{4,0},{1,9},{9... | collective-permute-start | bytes 983048 | tf_op jit(solution)/shard_map/ppermute | solution.py:118
  176.3 17.6 %collective-permute-start.30 = (bf16[128,1280]{1,0:T(8,128)(2,1)S(1)}, bf16[128,1280]{1,0:T(8,128)(2,1)S(1)}, u32[]{:S(2)}, u32[]{:S(2)}) collective-permute-start(bf16[128,1280]{1,0:T(8,128)(2,1)S(1)} %collective-permute-done.29.refs_2_), channel_id=1, source_target_pairs={{8,0},{16,8},{24,16},{28,24},{20,28},{12,20},{4,12},{0,4},{9,1},{1... | collective-permute-start | bytes 983048 | tf_op jit(solution)/shard_map/ppermute | solution.py:119
  187.2 13.7 %collective-permute-start.26 = (bf16[128,896]{1,0:T(8,128)(2,1)}, bf16[128,896]{1,0:T(8,128)(2,1)}, u32[]{:S(2)}, u32[]{:S(2)}) collective-permute-start(bf16[128,896]{1,0:T(8,128)(2,1)} %slice.114), channel_id=1, source_target_pairs={{0,8},{8,16},{16,24},{24,28},{28,20},{20,12},{12,4},{4,0},{1,9},{9... | collective-permute-start | bytes 688136 | tf_op jit(solution)/shard_map/ppermute | solution.py:123
  189.1 11.8 %collective-permute-start.27 = (bf16[128,896]{1,0:T(8,128)(2,1)}, bf16[128,896]{1,0:T(8,128)(2,1)}, u32[]{:S(2)}, u32[]{:S(2)}) collective-permute-start(bf16[128,896]{1,0:T(8,128)(2,1)} %slice.115), channel_id=1, source_target_pairs={{8,0},{16,8},{24,16},{28,24},{20,28},{12,20},{4,12},{0,4},{9,1},{1... | collective-permute-start | bytes 688136 | tf_op jit(solution)/shard_map/ppermute | solution.py:124
  193.4 11.5 %collective-permute-start.34 = (bf16[128,640]{1,0:T(8,128)(2,1)}, bf16[128,640]{1,0:T(8,128)(2,1)}, u32[]{:S(2)}, u32[]{:S(2)}) collective-permute-start(bf16[128,640]{1,0:T(8,128)(2,1)} %slice.118), channel_id=1, source_target_pairs={{0,8},{8,16},{16,24},{24,28},{28,20},{20,12},{12,4},{4,0},{1,9},{9... | collective-permute-start | bytes 491528 | tf_op jit(solution)/shard_map/ppermute | solution.py:123
  195.3 9.6 %collective-permute-start.35 = (bf16[128,640]{1,0:T(8,128)(2,1)}, bf16[128,640]{1,0:T(8,128)(2,1)}, u32[]{:S(2)}, u32[]{:S(2)}) collective-permute-start(bf16[128,640]{1,0:T(8,128)(2,1)} %slice.119), channel_id=1, source_target_pairs={{8,0},{16,8},{24,16},{28,24},{20,28},{12,20},{4,12},{0,4},{9,1},{1... | collective-permute-start | bytes 491528 | tf_op jit(solution)/shard_map/ppermute | solution.py:124
  282.5 14.7 %collective-permute-start.37 = (bf16[2,1024,256]{2,1,0:T(8,128)(2,1)S(1)}, bf16[2,1024,256]{2,1,0:T(8,128)(2,1)S(1)}, u32[]{:S(2)}, u32[]{:S(2)}) collective-permute-start(bf16[2,1024,256]{2,1,0:T(8,128)(2,1)S(1)} %constant_dynamic-slice_fusion.4), channel_id=1, source_target_pairs={{0,1},{1,0},{2,3},{3,2},{4,5},{5,4},{6,7},{7,6},{8,9},{9,8},{10,11... | collective-permute-start | bytes 3145736 | tf_op jit(solution)/shard_map/ppermute | solution.py:192
  282.7 14.3 %collective-permute-start.41 = (bf16[1,1024,256]{2,1,0:T(8,128)(2,1)S(1)}, bf16[1,1024,256]{2,1,0:T(8,128)(2,1)S(1)}, u32[]{:S(2)}, u32[]{:S(2)}) collective-permute-start(bf16[1,1024,256]{2,1,0:T(8,128)(2,1)S(1)} %copy-done.22), channel_id=1, source_target_pairs={{0,2},{1,3},{2,0},{3,1},{4,6},{5,7},{6,4},{7,5},{8,10},{9,11},{10,... | collective-permute-start | bytes 1572872 | tf_op jit(solution)/shard_map/ppermute | solution.py:192
  297.5 13.6 %collective-permute-start.38 = (bf16[1,1024,256]{2,1,0:T(8,128)(2,1)S(1)}, bf16[1,1024,256]{2,1,0:T(8,128)(2,1)S(1)}, u32[]{:S(2)}, u32[]{:S(2)}) collective-permute-start(bf16[1,1024,256]{2,1,0:T(8,128)(2,1)S(1)} %dynamic-slice_convert_fusion.1), channel_id=1, source_target_pairs={{0,2},{1,3},{2,0},{3,1},{4,6},{5,7},{6,4},{7,5},{8,10},{9,11},{10,... | collective-permute-start | bytes 1572872 | tf_op jit(solution)/shard_map/ppermute | solution.py:192
  313.5 12.8 %collective-permute-start.42 = (bf16[1,1024,256]{2,1,0:T(8,128)(2,1)S(1)}, bf16[1,1024,256]{2,1,0:T(8,128)(2,1)S(1)}, u32[]{:S(2)}, u32[]{:S(2)}) collective-permute-start(bf16[1,1024,256]{2,1,0:T(8,128)(2,1)S(1)} %get-tuple-element.124), channel_id=1, source_target_pairs={{0,2},{1,3},{2,0},{3,1},{4,6},{5,7},{6,4},{7,5},{8,10},{9,11},{10,... | collective-permute-start | bytes 1572872 | tf_op jit(solution)/shard_map/ppermute | solution.py:210
  378.2 3.7 collective-permute-start.44
  384.6 26.6 %collective-permute-start.45 = (bf16[1,1024,256]{2,1,0:T(8,128)(2,1)}, bf16[1,1024,256]{2,1,0:T(8,128)(2,1)S(1)}, u32[]{:S(2)}, u32[]{:S(2)}) collective-permute-start(bf16[1,1024,256]{2,1,0:T(8,128)(2,1)} %dynamic-slice_convert_fusion), channel_id=1, source_target_pairs={{0,2},{1,3},{2,0},{3,1},{4,6},{5,7},{6,4},{7,5},{8,10},{9,11},{10,... | collective-permute-start | bytes 1572872 | tf_op jit(solution)/shard_map/ppermute | solution.py:192
  385.0 13.7 %collective-permute-start.56 = (bf16[128,1152]{1,0:T(8,128)(2,1)S(1)}, bf16[128,1152]{1,0:T(8,128)(2,1)S(1)}, u32[]{:S(2)}, u32[]{:S(2)}) collective-permute-start(bf16[128,1152]{1,0:T(8,128)(2,1)S(1)} %get-tuple-element.133), channel_id=1, source_target_pairs={{0,8},{8,16},{16,24},{24,28},{28,20},{20,12},{12,4},{4,0},{1,9},{9... | collective-permute-start | bytes 884744 | tf_op jit(solution)/shard_map/ppermute | solution.py:161
  385.1 20.3 %collective-permute-start.57 = (bf16[128,1152]{1,0:T(8,128)(2,1)S(1)}, bf16[128,1152]{1,0:T(8,128)(2,1)}, u32[]{:S(2)}, u32[]{:S(2)}) collective-permute-start(bf16[128,1152]{1,0:T(8,128)(2,1)S(1)} %get-tuple-element.132), channel_id=1, source_target_pairs={{8,0},{16,8},{24,16},{28,24},{20,28},{12,20},{4,12},{0,4},{9,1},{1... | collective-permute-start | bytes 884744 | tf_op jit(solution)/shard_map/ppermute | solution.py:162
  387.0 29.6 %collective-permute-start.39 = (bf16[1,1024,256]{2,1,0:T(8,128)(2,1)}, bf16[1,1024,256]{2,1,0:T(8,128)(2,1)}, u32[]{:S(2)}, u32[]{:S(2)}) collective-permute-start(bf16[1,1024,256]{2,1,0:T(8,128)(2,1)} %get-tuple-element.131), channel_id=1, source_target_pairs={{0,2},{1,3},{2,0},{3,1},{4,6},{5,7},{6,4},{7,5},{8,10},{9,11},{10,... | collective-permute-start | bytes 1572872 | tf_op jit(solution)/shard_map/ppermute | solution.py:210
  409.1 23.2 %collective-permute-start.58 = (bf16[128,2304]{1,0:T(8,128)(2,1)}, bf16[128,2304]{1,0:T(8,128)(2,1)}, u32[]{:S(2)}, u32[]{:S(2)}) collective-permute-start(bf16[128,2304]{1,0:T(8,128)(2,1)} %get-tuple-element.107), channel_id=1, source_target_pairs={{0,8},{8,16},{16,24},{24,28},{28,20},{20,12},{12,4},{4,0},{1,9},{9... | collective-permute-start | bytes 1769480 | tf_op jit(solution)/shard_map/ppermute | solution.py:166
  410.6 21.8 %collective-permute-start.59 = (bf16[128,2304]{1,0:T(8,128)(2,1)}, bf16[128,2304]{1,0:T(8,128)(2,1)}, u32[]{:S(2)}, u32[]{:S(2)}) collective-permute-start(bf16[128,2304]{1,0:T(8,128)(2,1)} %get-tuple-element.108), channel_id=1, source_target_pairs={{8,0},{16,8},{24,16},{28,24},{20,28},{12,20},{4,12},{0,4},{9,1},{1... | collective-permute-start | bytes 1769480 | tf_op jit(solution)/shard_map/ppermute | solution.py:167
  412.8 25.0 %collective-permute-start.46 = (bf16[1,1024,256]{2,1,0:T(8,128)(2,1)}, bf16[1,1024,256]{2,1,0:T(8,128)(2,1)S(1)}, u32[]{:S(2)}, u32[]{:S(2)}) collective-permute-start(bf16[1,1024,256]{2,1,0:T(8,128)(2,1)} %fusion.11), channel_id=1, source_target_pairs={{0,2},{1,3},{2,0},{3,1},{4,6},{5,7},{6,4},{7,5},{8,10},{9,11},{10,... | collective-permute-start | bytes 1572872 | tf_op jit(solution)/shard_map/ppermute | solution.py:210
  415.2 12.1 %collective-permute-start.48 = (bf16[144,384]{1,0:T(8,128)(2,1)S(1)}, bf16[144,384]{1,0:T(8,128)(2,1)S(1)}, u32[]{:S(2)}, u32[]{:S(2)}) collective-permute-start(bf16[144,384]{1,0:T(8,128)(2,1)S(1)} %get-tuple-element.135), channel_id=1, source_target_pairs={{0,8},{8,16},{16,24},{24,28},{28,20},{20,12},{12,4},{4,0},{1,9},{9... | collective-permute-start | bytes 331784 | tf_op jit(solution)/shard_map/ppermute | solution.py:161
  416.7 11.2 %collective-permute-start.49 = (bf16[144,384]{1,0:T(8,128)(2,1)S(1)}, bf16[144,384]{1,0:T(8,128)(2,1)S(1)}, u32[]{:S(2)}, u32[]{:S(2)}) collective-permute-start(bf16[144,384]{1,0:T(8,128)(2,1)S(1)} %get-tuple-element.134), channel_id=1, source_target_pairs={{8,0},{16,8},{24,16},{28,24},{20,28},{12,20},{4,12},{0,4},{9,1},{1... | collective-permute-start | bytes 331784 | tf_op jit(solution)/shard_map/ppermute | solution.py:162
  427.3 62.2 %collective-permute-start.40 = (bf16[2,1024,256]{2,1,0:T(8,128)(2,1)S(1)}, bf16[2,1024,256]{2,1,0:T(8,128)(2,1)S(1)}, u32[]{:S(2)}, u32[]{:S(2)}) collective-permute-start(bf16[2,1024,256]{2,1,0:T(8,128)(2,1)S(1)} %maximum_select_fusion.5), channel_id=1, source_target_pairs={{0,1},{1,0},{2,3},{3,2},{4,5},{5,4},{6,7},{7,6},{8,9},{9,8},{10,11... | collective-permute-start | bytes 3145736 | tf_op jit(solution)/shard_map/ppermute | solution.py:210
  431.2 8.9 %collective-permute-start.50 = (bf16[144,768]{1,0:T(8,128)(2,1)}, bf16[144,768]{1,0:T(8,128)(2,1)S(1)}, u32[]{:S(2)}, u32[]{:S(2)}) collective-permute-start(bf16[144,768]{1,0:T(8,128)(2,1)} %get-tuple-element.99), channel_id=1, source_target_pairs={{0,8},{8,16},{16,24},{24,28},{28,20},{20,12},{12,4},{4,0},{1,9},{9... | collective-permute-start | bytes 663560 | tf_op jit(solution)/shard_map/ppermute | solution.py:166
  435.8 25.6 %collective-permute-start.60 = (bf16[128,2304]{1,0:T(8,128)(2,1)}, bf16[128,2304]{1,0:T(8,128)(2,1)S(1)}, u32[]{:S(2)}, u32[]{:S(2)}) collective-permute-start(bf16[128,2304]{1,0:T(8,128)(2,1)} %get-tuple-element.109), channel_id=1, source_target_pairs={{0,8},{8,16},{16,24},{24,28},{28,20},{20,12},{12,4},{4,0},{1,9},{9... | collective-permute-start | bytes 1769480 | tf_op jit(solution)/shard_map/ppermute | solution.py:166
  437.5 23.8 %collective-permute-start.61 = (bf16[128,2304]{1,0:T(8,128)(2,1)}, bf16[128,2304]{1,0:T(8,128)(2,1)S(1)}, u32[]{:S(2)}, u32[]{:S(2)}) collective-permute-start(bf16[128,2304]{1,0:T(8,128)(2,1)} %get-tuple-element.110), channel_id=1, source_target_pairs={{8,0},{16,8},{24,16},{28,24},{20,28},{12,20},{4,12},{0,4},{9,1},{1... | collective-permute-start | bytes 1769480 | tf_op jit(solution)/shard_map/ppermute | solution.py:167
  440.1 59.7 %collective-permute-start.47 = (bf16[2,1024,256]{2,1,0:T(8,128)(2,1)}, bf16[2,1024,256]{2,1,0:T(8,128)(2,1)}, u32[]{:S(2)}, u32[]{:S(2)}) collective-permute-start(bf16[2,1024,256]{2,1,0:T(8,128)(2,1)} %maximum_select_fusion.7), channel_id=1, source_target_pairs={{0,1},{1,0},{2,3},{3,2},{4,5},{5,4},{6,7},{7,6},{8,9},{9,8},{10,11... | collective-permute-start | bytes 3145736 | tf_op jit(solution)/shard_map/ppermute | solution.py:210
  440.2 16.0 %collective-permute-start.51 = (bf16[144,768]{1,0:T(8,128)(2,1)S(1)}, bf16[144,768]{1,0:T(8,128)(2,1)S(1)}, u32[]{:S(2)}, u32[]{:S(2)}) collective-permute-start(bf16[144,768]{1,0:T(8,128)(2,1)S(1)} %copy-done.52), channel_id=1, source_target_pairs={{8,0},{16,8},{24,16},{28,24},{20,28},{12,20},{4,12},{0,4},{9,1},{1... | collective-permute-start | bytes 663560 | tf_op jit(solution)/shard_map/ppermute | solution.py:167
  459.6 8.8 %collective-permute-start.52 = (bf16[144,768]{1,0:T(8,128)(2,1)}, bf16[144,768]{1,0:T(8,128)(2,1)S(1)}, u32[]{:S(2)}, u32[]{:S(2)}) collective-permute-start(bf16[144,768]{1,0:T(8,128)(2,1)} %get-tuple-element.101), channel_id=1, source_target_pairs={{0,8},{8,16},{16,24},{24,28},{28,20},{20,12},{12,4},{4,0},{1,9},{9... | collective-permute-start | bytes 663560 | tf_op jit(solution)/shard_map/ppermute | solution.py:166
  466.4 30.1 %collective-permute-start.62 = (bf16[128,2304]{1,0:T(8,128)(2,1)}, bf16[128,2304]{1,0:T(8,128)(2,1)}, u32[]{:S(2)}, u32[]{:S(2)}) collective-permute-start(bf16[128,2304]{1,0:T(8,128)(2,1)} %get-tuple-element.111), channel_id=1, source_target_pairs={{0,8},{8,16},{16,24},{24,28},{28,20},{20,12},{12,4},{4,0},{1,9},{9... | collective-permute-start | bytes 1769480 | tf_op jit(solution)/shard_map/ppermute | solution.py:166
  467.2 29.3 %collective-permute-start.63 = (bf16[128,2304]{1,0:T(8,128)(2,1)}, bf16[128,2304]{1,0:T(8,128)(2,1)}, u32[]{:S(2)}, u32[]{:S(2)}) collective-permute-start(bf16[128,2304]{1,0:T(8,128)(2,1)} %get-tuple-element.112), channel_id=1, source_target_pairs={{8,0},{16,8},{24,16},{28,24},{20,28},{12,20},{4,12},{0,4},{9,1},{1... | collective-permute-start | bytes 1769480 | tf_op jit(solution)/shard_map/ppermute | solution.py:167
  468.4 16.9 %collective-permute-start.53 = (bf16[144,768]{1,0:T(8,128)(2,1)S(1)}, bf16[144,768]{1,0:T(8,128)(2,1)S(1)}, u32[]{:S(2)}, u32[]{:S(2)}) collective-permute-start(bf16[144,768]{1,0:T(8,128)(2,1)S(1)} %copy-done.51), channel_id=1, source_target_pairs={{8,0},{16,8},{24,16},{28,24},{20,28},{12,20},{4,12},{0,4},{9,1},{1... | collective-permute-start | bytes 663560 | tf_op jit(solution)/shard_map/ppermute | solution.py:167
  488.7 20.4 %collective-permute-start.54 = (bf16[144,768]{1,0:T(8,128)(2,1)}, bf16[144,768]{1,0:T(8,128)(2,1)S(1)}, u32[]{:S(2)}, u32[]{:S(2)}) collective-permute-start(bf16[144,768]{1,0:T(8,128)(2,1)} %get-tuple-element.103), channel_id=1, source_target_pairs={{0,8},{8,16},{16,24},{24,28},{28,20},{20,12},{12,4},{4,0},{1,9},{9... | collective-permute-start | bytes 663560 | tf_op jit(solution)/shard_map/ppermute | solution.py:166
  490.5 18.7 %collective-permute-start.55 = (bf16[144,768]{1,0:T(8,128)(2,1)}, bf16[144,768]{1,0:T(8,128)(2,1)}, u32[]{:S(2)}, u32[]{:S(2)}) collective-permute-start(bf16[144,768]{1,0:T(8,128)(2,1)} %get-tuple-element.104), channel_id=1, source_target_pairs={{8,0},{16,8},{24,16},{28,24},{20,28},{12,20},{4,12},{0,4},{9,1},{1... | collective-permute-start | bytes 663560 | tf_op jit(solution)/shard_map/ppermute | solution.py:167
  517.2 4.6 collective-permute-start.66
  517.2 4.6 collective-permute-start.65
  (58 other events, 482.2 us)
Sparse Core Ops, SparseCore 0:
  274.3 132.1 reduce-scatter.1
